TPU v7x, 32 devices: a whole 2x2x4 slice. The times are simulated.
32 devices in a mesh: tok: 16 (over z, x, core), ffn: 2 (over y).
Axes of the slice: x: 2, y: 2, z: 4, core: 2. Of those that a mesh axis runs over, the one named last changes fastest.
Arguments:
- tokens: bfloat16 [16384, 768], P(('tok', 'ffn')), may hold values from -6 to 6
- rel_ids: int32 [32, 512, 512], P(('tok', 'ffn')), may hold values from 1 to 511, as said below
- mask_pos: int32 [32, 80], P(('tok', 'ffn')), may hold values from -1 to 511, as said below
- grad_vals: bfloat16 [32, 80, 768], P(('tok', 'ffn')), may hold values from -6 to 6
- w_query: bfloat16 [768, 768], replicated, may hold values from -0.21875 to 0.21875
- w_key: bfloat16 [768, 768], replicated, may hold values from -0.21875 to 0.21875
- w_value: bfloat16 [768, 768], replicated, may hold values from -0.21875 to 0.21875
- w_out: bfloat16 [768, 768], replicated, may hold values from -3 to 3
- b_query: float32 [768], replicated, may hold values from -3 to 3
- b_key: float32 [768], replicated, may hold values from -3 to 3
- b_value: float32 [768], replicated, may hold values from -3 to 3
- b_out: float32 [768], replicated, may hold values from -3 to 3
- rel_table: bfloat16 [512, 768], replicated, may hold values from -6 to 6
- ln1_gain: float32 [768], replicated, may hold values from 0.5 to 1.5
- ln1_bias: float32 [768], replicated, may hold values from -2 to 2
- w_in: bfloat16 [768, 3072], P(None, 'ffn'), may hold values from -0.21875 to 0.21875
- b_in: float32 [3072], P('ffn'), may hold values from -3 to 3
- w_down: bfloat16 [3072, 768], P('ffn'), may hold values from -0.109375 to 0.109375
- b_down: float32 [768], replicated, may hold values from -2 to 2
- ln2_gain: float32 [768], replicated, may hold values from 0.5 to 1.5
- ln2_bias: float32 [768], replicated, may hold values from -2 to 2
Outputs:
- output: bfloat16 [16384, 768], P(('tok', 'ffn'))
- grad_tokens: float32 [16384, 768], P(('tok', 'ffn'))
- grad_w_query: float32 [768, 768], P(('tok', 'ffn'))
- grad_w_key: float32 [768, 768], P(('tok', 'ffn'))
- grad_w_value: float32 [768, 768], P(('tok', 'ffn'))
- grad_w_out: float32 [768, 768], P(('tok', 'ffn'))
- grad_b_query: float32 [768], P(('tok', 'ffn'))
- grad_b_key: float32 [768], P(('tok', 'ffn'))
- grad_b_value: float32 [768], P(('tok', 'ffn'))
- grad_b_out: float32 [768], P(('tok', 'ffn'))
- grad_rel_table: float32 [512, 768], P(('tok', 'ffn'))
- grad_ln1_gain: float32 [768], P(('tok', 'ffn'))
- grad_ln1_bias: float32 [768], P(('tok', 'ffn'))
- grad_w_in: float32 [768, 3072], P('tok', 'ffn')
- grad_b_in: float32 [2, 1536], P('ffn', 'tok')
- grad_w_down: float32 [3072, 768], P('ffn', 'tok')
- grad_b_down: float32 [768], P(('tok', 'ffn'))
- grad_ln2_gain: float32 [768], P(('tok', 'ffn'))
- grad_ln2_bias: float32 [768], P(('tok', 'ffn'))
Inputs may be any that keep to these rules, and one draw needn't show every extreme that they name: `mask_pos`: row s names distinct positions of sequence s in its first slots and -1 in the others; each row names 64 to 80 positions, and some row names 80. rel_ids[s, i, j] = 256 + the DeBERTa log bucket (identity up to 128, logarithmic beyond, maximum position 512) of p_i - p_j, where p_i counts word starts before token i of sequence s, tokens of one word sharing it; so rel_ids[s, j, i] = 512 - rel_ids[s, i, j].
All inputs are finite; a program needn't handle non-finite values.
Results may differ from a plain program's by a relative error of at most 0.034.
Values may be sent and summed in bfloat16 or wider, within the bound.
No kernel may reach another device: no remote copies, remote signals or barrier semaphores. Data moves between devices by JAX's collectives and lax.ppermute only.
A program may use at most 256 MiB of HBM per device.

v0:
```python
import functools
import math

import numpy as np

import jax
import jax.numpy as jnp
from jax import lax
from jax.experimental import pallas as pl
from jax.experimental.pallas import tpu as pltpu
from jax.sharding import PartitionSpec as P

HEAD = 64
LANES = 128
HALF = 64
ROWS = 32
AT_ONCE = 2
FIRST_PAIRS = 2
VECTORS = 9
norm_eps = 1e-07
bf16 = jnp.bfloat16
f32 = jnp.float32
PARAMS = pltpu.CompilerParams(vmem_limit_bytes=60 * 2**20)


def dot_nn(first_op, second_op):
    return lax.dot_general(
        first_op, second_op, (((1,), (0,)), ((), ())), preferred_element_type=f32
    )


def dot_nt(first_op, second_op):
    return lax.dot_general(
        first_op, second_op, (((1,), (1,)), ((), ())), preferred_element_type=f32
    )


def dot_tn(first_op, second_op):
    return lax.dot_general(
        first_op, second_op, (((0,), (0,)), ((), ())), preferred_element_type=f32
    )


def distance_rows(seq_len, table_rows):
    side = table_rows // 2
    middle = side // 2
    rows = []
    for m in range(2 * seq_len):
        offset = max(m - seq_len, 1 - seq_len)
        size = abs(offset)
        if size > middle:
            ratio = math.log(size / middle) / math.log((2 * side - 1) / middle)
            size = int(math.ceil(ratio * (middle - 1))) + middle
        rows.append(side + (size if offset > 0 else -size))
    return np.array(rows, dtype=np.int32)


def lane_iota(rows=1):
    return lax.broadcasted_iota(jnp.int32, (rows, LANES), 1)


def member_chunk(words, c, last):
    return (last - words == lane_iota(words.shape[0]) + c * LANES).astype(f32).astype(bf16)


def id_bases(rel_ref, base):
    seq = rel_ref.shape[0]
    chunks = seq // LANES
    last = chunks * 2 - 2
    for g in range(seq // HALF):
        for c in range(chunks):
            block = rel_ref[g * HALF : (g + 1) * HALF, c * LANES : (c + 1) * LANES]
            base[g * chunks + c] = jnp.minimum(jnp.min(block) // HALF, last)


def both_alignments(table):
    return jnp.concatenate([table, table[HALF:], table[:HALF]], axis=0)


def longest(rows):
    wide = rows.astype(f32)
    return jnp.sqrt(jnp.max(jnp.sum(wide * wide, axis=1, keepdims=True)))


def pack_heads(first, second, dest, top):
    top = jnp.maximum(top, 1e-30)
    scale = 32000.0 / top
    upper = (first * scale).astype(jnp.int32)
    lower = (second * scale).astype(jnp.int32)
    dest[...] = upper * 65536 + lower
    return top * (1.0 / 32000.0)


def unpack_heads(words, step):
    lower = lax.shift_right_arithmetic(lax.shift_left(words, 16), 16)
    return words.astype(f32) * (step * (1.0 / 65536.0)), lower.astype(f32) * step


def picked_words(source, rel_ref, base, rows, c):
    chunks = rel_ref.shape[1] // LANES
    first = base[(rows.start // HALF) * chunks + c]
    place = rel_ref[rows, c * LANES : (c + 1) * LANES] - first * HALF
    index = place & (LANES - 1)
    at = pl.multiple_of((first % 2) * (chunks * LANES) + (first // 2) * LANES, LANES)
    near = jnp.take_along_axis(source[rows, pl.ds(at, LANES)], index, axis=1)
    at = pl.multiple_of(at + LANES, LANES)
    far = jnp.take_along_axis(source[rows, pl.ds(at, LANES)], index, axis=1)
    return jnp.where(place < LANES, near, far)


def unshift_in_order(sources, words_ref, base, dest):
    seq = words_ref.shape[0]
    chunks = seq // LANES
    lane = lane_iota()
    zero = jnp.zeros((ROWS, LANES), f32)
    for g in range(chunks):
        first = base[g]
        for sub in range(LANES // ROWS):
            start = g * LANES + sub * ROWS
            rows = slice(start, start + ROWS)
            place = lane - 1 - words_ref[rows, :] + first * LANES
            index = place & (LANES - 1)
            near = place >= 0
            mid = place >= -LANES
            for a, source in enumerate(sources):
                turned = [
                    jnp.take_along_axis(
                        source[rows, c * LANES : (c + 1) * LANES], index, axis=1
                    )
                    for c in range(chunks)
                ]
                turned = [zero, zero] + turned + [zero, zero]
                for c in range(chunks + 2):
                    value = jnp.where(near, turned[c + 2], jnp.where(mid, turned[c + 1], turned[c]))
                    at = pl.multiple_of((first + c) * LANES, LANES)
                    dest[a, rows, pl.ds(at, LANES)] = value.astype(bf16)


def group_bases(words, base):
    seq = words.shape[0]
    for g in range(seq // LANES):
        base[g] = (jnp.min(words[g * LANES : (g + 1) * LANES]) + 1) // LANES


def softmax_weights(scores):
    factor = math.log2(math.e) / math.sqrt(3.0 * HEAD)
    top = jnp.max(functools.reduce(jnp.maximum, scores), axis=1, keepdims=True)
    return [jnp.exp2((score - top) * factor) for score in scores]


def head_lanes(a):
    return (lane_iota() < HEAD) if a == 0 else (lane_iota() >= HEAD)


def row_of(ref):
    return ref[...].reshape(1, ref.shape[0])


def norm_stats(values):
    centered = values - jnp.mean(values, axis=1, keepdims=True)
    inv_std = lax.rsqrt(jnp.mean(centered * centered, axis=1, keepdims=True) + norm_eps)
    return centered * inv_std, inv_std


def norm_backward(upstream, normed, inv_std, norm_gain):
    scaled = upstream * norm_gain
    adjusted = (
        scaled
        - jnp.mean(scaled, axis=1, keepdims=True)
        - normed * jnp.mean(scaled * normed, axis=1, keepdims=True)
    )
    return inv_std * adjusted, col_sum(upstream * normed), col_sum(upstream)


def col_sum(values):
    return jnp.sum(values, axis=0, keepdims=True)


def normal_cdf(pre_act):
    return 0.5 * (1.0 + lax.erf(pre_act * (1.0 / math.sqrt(2.0))))


def picked_kernel(
    pos_ref, rel_ref, qc_ref, k_ref, v_ref, pk_ref, pq_ref,
    x_ref, wo_ref, bo_ref, gain_ref, bias_ref,
    ctx_ref, prob_ref, key_ref, word_ref, wordc_ref, normed_ref, inv_ref, low_ref,
    packed, cpick, relc, keyc, attn, base,
):
    seq = k_ref.shape[0]
    picks = qc_ref.shape[0]
    chunks = seq // LANES

    @pl.when(pl.program_id(0) == 0)
    def _():
        row = lax.broadcasted_iota(jnp.int32, (seq, seq), 0)
        col = lax.broadcasted_iota(jnp.int32, (seq, seq), 1)
        side = pk_ref.shape[0] // 2
        step = jnp.sum(jnp.where(col == row - 1, rel_ref[...] - side, 0), axis=1, keepdims=True)
        steps = jnp.broadcast_to(step.astype(f32), (seq, LANES)).astype(bf16)
        word_ref[...] = dot_nn((col <= row).astype(f32).astype(bf16), steps).astype(jnp.int32)
        id_bases(rel_ref, base)
        for n in range(picks):
            place = jnp.maximum(pos_ref[n], 0)
            relc[n : n + 1, :] = rel_ref[pl.ds(place, 1), :]
            wordc_ref[n : n + 1, :] = word_ref[pl.ds(place, 1), :]

    zero = jnp.zeros((), bf16)
    table = both_alignments(pq_ref[...])
    keys = [dot_nt(jnp.where(head_lanes(a), k_ref[...], zero), table) for a in range(2)]
    unit = pack_heads(keys[0], keys[1], packed, longest(k_ref[...]) * longest(pq_ref[...]))
    for a in range(2):
        cpick[a] = dot_nt(jnp.where(head_lanes(a), qc_ref[...], zero), pk_ref[...])
    for g in range(chunks):
        for c in range(chunks):
            parts = []
            for start in range(g * LANES, (g + 1) * LANES, ROWS):
                parts.append(picked_words(packed, rel_ref, base, slice(start, start + ROWS), c))
            block = jnp.concatenate(parts, axis=0).T
            for a, value in enumerate(unpack_heads(block, unit)):
                key_ref[a, c * LANES : (c + 1) * LANES, g * LANES : (g + 1) * LANES] = value

    for n in range(picks):
        place = jnp.maximum(pos_ref[n], 0)
        for a in range(2):
            keyc[a, n : n + 1, :] = key_ref[a, pl.ds(place, 1), :]
    for a in range(2):
        mine = head_lanes(a)
        direct = dot_nt(jnp.where(mine, qc_ref[...], zero), k_ref[...])
        scores = []
        for c in range(chunks):
            ids = relc[:, c * LANES : (c + 1) * LANES]
            index = ids & (LANES - 1)
            value = jnp.take_along_axis(cpick[a, :, :LANES], index, axis=1)
            for n in range(1, pk_ref.shape[0] // LANES):
                other = cpick[a, :, n * LANES : (n + 1) * LANES]
                value = jnp.where(
                    ids >= n * LANES, jnp.take_along_axis(other, index, axis=1), value
                )
            cols = slice(c * LANES, (c + 1) * LANES)
            scores.append(direct[:, cols] + value + keyc[a, :, cols])
        weights = softmax_weights(scores)
        inverse = 1.0 / jnp.sum(sum(weights[1:], weights[0]), axis=1, keepdims=True)
        probs = jnp.concatenate([(weight * inverse).astype(bf16) for weight in weights], axis=1)
        prob_ref[a] = probs
        mixed = dot_nn(probs, v_ref[...]).astype(bf16)
        ctx_ref[...] = mixed if a == 0 else jnp.where(mine, mixed, ctx_ref[...])

    part = dot_nn(ctx_ref[...], wo_ref[...])

    @pl.when(pl.program_id(0) == 0)
    def _():
        attn[...] = x_ref[...].astype(f32) + row_of(bo_ref) + part

    @pl.when(pl.program_id(0) > 0)
    def _():
        attn[...] += part

    @pl.when(pl.program_id(0) == pl.num_programs(0) - 1)
    def _():
        normed, inv_std = norm_stats(attn[...])
        normed_ref[...] = normed
        inv_ref[...] = jnp.broadcast_to(inv_std, (picks, LANES))
        low_ref[...] = (normed * row_of(gain_ref) + row_of(bias_ref)).astype(bf16)


def attend_picked(
    positions, rel_ids, q_pick, k, v, pos_query, pos_key, x_pick, w_out, b_out, gain, bias
):
    seq, width = k.shape
    picks = q_pick.shape[0]
    table = pos_key.shape[0]
    pairs = width // LANES
    whole = lambda rows, cols: pl.BlockSpec((rows, cols), lambda h: (0, 0))
    line = pl.BlockSpec((width,), lambda h: (0,))
    col = lambda rows: pl.BlockSpec((rows, LANES), lambda h: (0, h))
    heads = lambda rows: pl.BlockSpec((2, rows, seq), lambda h: (h, 0, 0))
    return pl.pallas_call(
        picked_kernel,
        grid=(pairs,),
        in_specs=[
            pl.BlockSpec(memory_space=pltpu.SMEM), whole(seq, seq),
            col(picks), col(seq), col(seq), col(table), col(table),
            whole(picks, width), pl.BlockSpec((LANES, width), lambda h: (h, 0)), line, line, line,
        ],
        out_specs=[
            col(picks), heads(picks), heads(seq), whole(seq, LANES), whole(picks, LANES),
            whole(picks, width), whole(picks, LANES), whole(picks, width),
        ],
        out_shape=[
            jax.ShapeDtypeStruct((picks, width), bf16),
            jax.ShapeDtypeStruct((2 * pairs, picks, seq), bf16),
            jax.ShapeDtypeStruct((2 * pairs, seq, seq), f32),
            jax.ShapeDtypeStruct((seq, LANES), jnp.int32),
            jax.ShapeDtypeStruct((picks, LANES), jnp.int32),
            jax.ShapeDtypeStruct((picks, width), f32),
            jax.ShapeDtypeStruct((picks, LANES), f32),
            jax.ShapeDtypeStruct((picks, width), bf16),
        ],
        scratch_shapes=[
            pltpu.VMEM((seq, 2 * table), jnp.int32),
            pltpu.VMEM((2, picks, table), f32),
            pltpu.VMEM((picks, seq), jnp.int32),
            pltpu.VMEM((2, picks, seq), f32),
            pltpu.VMEM((picks, width), f32),
            pltpu.SMEM((seq // HALF * (seq // LANES),), jnp.int32),
        ],
        compiler_params=PARAMS,
        name="attend_picked",
    )(
        positions, rel_ids, q_pick, k, v, pos_key, pos_query, x_pick, w_out, b_out, gain, bias
    )


def full_kernel(rel_ref, q_ref, k_ref, v_ref, pk_ref, key_ref, ctx_ref, *scratch):
    seq = rel_ref.shape[0]
    chunks = seq // LANES
    base, scratch = scratch[-1], scratch[:-1]
    count = len(scratch) // 3

    @pl.when(pl.program_id(0) == 0)
    def _():
        id_bases(rel_ref, base)

    zero = jnp.zeros((), bf16)
    units = []
    for n in range(count):
        packed, direct, low = scratch[3 * n : 3 * n + 3]
        lanes = slice(n * LANES, (n + 1) * LANES)
        q, pos = q_ref[:, lanes], pk_ref[:, lanes]
        table = both_alignments(pos)
        far = []
        for a in range(2):
            q_a = jnp.where(head_lanes(a), q, zero)
            far.append(dot_nt(q_a, table))
            direct[a] = dot_nt(q_a, k_ref[:, lanes])
        units.append(pack_heads(far[0], far[1], packed, longest(q) * longest(pos)))
    for n in range(count):
        packed, direct, low = scratch[3 * n : 3 * n + 3]
        lanes = slice(n * LANES, (n + 1) * LANES)
        for start in range(0, seq, HALF):
            rows = slice(start, start + HALF)
            scores = [[], []]
            for c in range(chunks):
                cols = slice(c * LANES, (c + 1) * LANES)
                values = unpack_heads(picked_words(packed, rel_ref, base, rows, c), units[n])
                for a in range(2):
                    scores[a].append(
                        values[a] + direct[a, rows, cols] + key_ref[2 * n + a, rows, cols]
                    )
            for a in range(2):
                for c, weight in enumerate(softmax_weights(scores[a])):
                    low[a, rows, c * LANES : (c + 1) * LANES] = weight.astype(bf16)
        v = v_ref[:, lanes]
        mixed = [
            dot_nn(low[a], jnp.where(head_lanes(a), v, jnp.ones((), bf16))) for a in range(2)
        ]
        upper = head_lanes(0)
        totals = pltpu.roll(jnp.where(upper, mixed[1], mixed[0]), HEAD, 1)
        ctx_ref[:, lanes] = (jnp.where(upper, mixed[0], mixed[1]) * (1.0 / totals)).astype(bf16)


def attend_full(rel_ids, q, k, v, pos_key, key_scores, first, pairs):
    seq = k.shape[0]
    table = pos_key.shape[0]
    per = AT_ONCE
    wide = per * LANES
    col = lambda rows: pl.BlockSpec((rows, wide), lambda h: (0, h + first // per))
    return pl.pallas_call(
        full_kernel,
        grid=(pairs // per,),
        in_specs=[
            pl.BlockSpec((seq, seq), lambda h: (0, 0)),
            col(seq), col(seq), col(seq), col(table),
            pl.BlockSpec((2 * per, seq, seq), lambda h: (h + first // per, 0, 0)),
        ],
        out_specs=pl.BlockSpec((seq, wide), lambda h: (0, h)),
        out_shape=jax.ShapeDtypeStruct((seq, pairs * LANES), bf16),
        scratch_shapes=[
            pltpu.VMEM((seq, 2 * table), jnp.int32),
            pltpu.VMEM((2, seq, seq), f32),
            pltpu.VMEM((2, seq, seq), bf16),
        ]
        * per
        + [pltpu.SMEM((seq // HALF * (seq // LANES),), jnp.int32)],
        compiler_params=PARAMS,
        name="attend_full",
    )(rel_ids, q, k, v, pos_key, key_scores)


def back_kernel(
    row_ref, word_ref, wordc_ref, qc_ref, k_ref, v_ref, prob_ref, pk_ref, pq_ref,
    dz2_ref, mine_ref, got_ref, normed_ref, inv_ref, gain_ref, wo_ref, early_ref,
    dq_ref, dk_ref, dv_ref, dpos_ref, dz1_ref, dattn_ref, sum_ref,
    side, sidec, moved, movedc, expand, shrink, base,
):
    seq = k_ref.shape[0]
    picks = qc_ref.shape[0]
    table = pk_ref.shape[0]
    chunks = seq // LANES

    @pl.when(pl.program_id(0) == 0)
    def _():
        words = word_ref[...]
        for c in range(chunks):
            side[:, c * LANES : (c + 1) * LANES] = member_chunk(words, c, seq - 1)
            sidec[:, c * LANES : (c + 1) * LANES] = member_chunk(wordc_ref[...], c, seq - 1)
        group_bases(words, base)
        moved[...] = jnp.zeros_like(moved)
        edge = expand.shape[1]
        for n, start in ((0, 0), (1, 2 * seq - edge)):
            ids = row_ref[start : start + edge, :] - n * (table - LANES)
            chosen = (ids == lane_iota(edge)).astype(f32).astype(bf16)
            expand[n] = chosen
            shrink[n] = chosen.T
        dh1 = dz2_ref[...] + mine_ref[...].astype(f32) + got_ref[...].astype(f32)
        dz1, g_gain, g_bias = norm_backward(dh1, normed_ref[...], inv_ref[:, :1], row_of(gain_ref))
        dz1_ref[...] = dz1
        dattn = dz1.astype(bf16)
        dattn_ref[...] = dattn
        sum_ref[...] = jnp.concatenate(
            [col_sum(dattn.astype(f32)), g_gain, g_bias, early_ref[:5]], axis=0
        )

    lane = lane_iota()
    scale = 1.0 / math.sqrt(3.0 * HEAD)
    zero = jnp.zeros((), bf16)
    heads = range(2)
    upper = head_lanes(0)
    join = lambda pair: jnp.where(upper, pair[0], pair[1])
    side[:, seq:] = k_ref[...]
    sidec[:, seq:] = qc_ref[...]
    dctx = dot_nt(dattn_ref[...], wo_ref[...]).astype(bf16)
    dprobs = [dot_nt(jnp.where(head_lanes(a), dctx, zero), v_ref[...]) for a in heads]

    def widened(ref):
        ends = [
            dot_nn(expand[n], ref[at : at + LANES, :]).astype(bf16)
            for n, at in ((0, 0), (1, table - LANES))
        ]
        return jnp.concatenate([ends[0], ref[LANES : table - LANES, :], ends[1]], axis=0)

    far_key, far_query = widened(pk_ref), widened(pq_ref)
    gs = []
    for a in heads:
        probs = prob_ref[a].astype(f32)
        prod = probs * dprobs[a]
        gs.append(((prod - probs * jnp.sum(prod, axis=1, keepdims=True)) * scale).astype(bf16))
    outs = [dot_tn(gs[a], sidec[...]) for a in heads]
    outcs = [dot_nn(gs[a], side[...]) for a in heads]
    dv_ref[...] = join([dot_tn(prob_ref[a], dctx) for a in heads]).astype(bf16)
    place = lane - 1 - wordc_ref[...]
    index = place & (LANES - 1)
    blank = jnp.zeros((picks, LANES), f32)
    for a in heads:
        turned = [
            jnp.take_along_axis(outcs[a][:, c * LANES : (c + 1) * LANES], index, axis=1)
            for c in range(chunks)
        ]
        for c in range(2 * chunks):
            value = turned[c] if c < chunks else blank
            for n in range(1, chunks + 1):
                other = turned[c - n] if 0 <= c - n < chunks else blank
                value = jnp.where(place < -LANES * (n - 1), other, value)
            movedc[a, :, c * LANES : (c + 1) * LANES] = value.astype(bf16)
    unshift_in_order(outs, word_ref, base, moved)
    dq = [outcs[a][:, seq:] + dot_nn(movedc[a], far_key) for a in heads]
    dq_ref[...] = join(dq).astype(bf16)
    dk = [outs[a][:, seq:] + dot_nn(moved[a, :, : 2 * seq], far_query) for a in heads]
    dk_ref[...] = join(dk).astype(bf16)
    far = [
        join([dot_tn(movedc[a], qc_ref[...]) for a in heads]),
        join([dot_tn(moved[a, :, : 2 * seq], k_ref[...]) for a in heads]),
    ]
    edge = expand.shape[1]
    for n, value in enumerate(far):
        value = value.astype(bf16)
        dpos_ref[n, :LANES, :] = dot_nn(shrink[0], value[:edge]).astype(bf16)
        dpos_ref[n, LANES : table - LANES, :] = value[edge : 2 * seq - edge]
        dpos_ref[n, table - LANES :, :] = dot_nn(shrink[1], value[2 * seq - edge :]).astype(bf16)


def attend_back(
    table_of, words, words_pick, q_pick, k, v, probs, pos_query, pos_key,
    dz2, mine, got, normed, inv_std, gain, w_out, early,
):
    seq, width = k.shape
    picks = q_pick.shape[0]
    table = pos_key.shape[0]
    pairs = width // LANES
    edge = seq - table // 4
    whole = lambda value: pl.BlockSpec(value.shape, lambda h: (0,) * value.ndim)
    col = lambda rows: pl.BlockSpec((rows, LANES), lambda h: (0, h))
    shape = lambda rows: jax.ShapeDtypeStruct((rows, width), bf16)
    return pl.pallas_call(
        back_kernel,
        grid=(pairs,),
        in_specs=[
            whole(table_of), whole(words), whole(words_pick),
            col(picks), col(seq), col(seq),
            pl.BlockSpec((2, picks, seq), lambda h: (h, 0, 0)),
            col(table), col(table),
            whole(dz2), whole(mine), whole(got), whole(normed), whole(inv_std), whole(gain),
            pl.BlockSpec((LANES, width), lambda h: (h, 0)), whole(early),
        ],
        out_specs=[
            col(picks), col(seq), col(seq),
            pl.BlockSpec((2, table, LANES), lambda h: (0, 0, h)),
            whole(dz2), whole(dz2), whole(early),
        ],
        out_shape=[
            shape(picks), shape(seq), shape(seq),
            jax.ShapeDtypeStruct((2, table, width), bf16),
            jax.ShapeDtypeStruct((picks, width), f32),
            shape(picks),
            jax.ShapeDtypeStruct(early.shape, f32),
        ],
        scratch_shapes=[
            pltpu.VMEM((seq, seq + LANES), bf16),
            pltpu.VMEM((picks, seq + LANES), bf16),
            pltpu.VMEM((2, seq, 2 * seq + 2 * LANES), bf16),
            pltpu.VMEM((2, picks, 2 * seq), bf16),
            pltpu.VMEM((2, edge, LANES), bf16),
            pltpu.VMEM((2, LANES, edge), bf16),
            pltpu.SMEM((seq // LANES,), jnp.int32),
        ],
        compiler_params=PARAMS,
        name="attend_back",
    )(
        table_of, words, words_pick, q_pick, k, v, probs, pos_key, pos_query,
        dz2, mine, got, normed, inv_std, gain, w_out, early,
    )


def turn_kernel(
    me_ref, order_ref, x_ref, xpick_ref, cpick_ref, rel_ref, x_out, xpick_out, cpick_out, rel_out
):
    picked = order_rows(order_ref, me_ref, x_ref.shape[1])
    for ref, out in ((x_ref, x_out), (xpick_ref, xpick_out), (cpick_ref, cpick_out), (rel_ref, rel_out)):
        out[...] = dot_nt(picked, ref[...]).astype(bf16)


def block_rows(ref, me_ref):
    return me_ref[0] ^ jnp.where(me_ref[1] == 0, ref[:, 0:1], ref[:, 1:2])


def order_rows(ref, me_ref, length):
    source = block_rows(ref, me_ref) * (length // me_ref[2]) + ref[:, 2:3]
    spot = lax.broadcasted_iota(jnp.int32, (ref.shape[0], length), 1)
    return (spot == source).astype(f32).astype(bf16)


def turn_blocks(me, order, x, x_pick, ctx_pick, rel_table):
    width = x.shape[1]
    group = 2 * LANES
    whole = lambda value: pl.BlockSpec(value.shape, lambda n: (0, 0))
    row = lambda count: pl.BlockSpec((group, count), lambda n: (n, 0))
    given = [x, x_pick, ctx_pick, rel_table]
    return pl.pallas_call(
        turn_kernel,
        grid=(width // group,),
        in_specs=[pl.BlockSpec(memory_space=pltpu.SMEM), row(LANES)]
        + [whole(value) for value in given],
        out_specs=[row(value.shape[0]) for value in given],
        out_shape=[jax.ShapeDtypeStruct(value.shape[::-1], bf16) for value in given],
        compiler_params=PARAMS,
        name="turn_blocks",
    )(me, order, *given)


def norm_picked_kernel(
    normed_ref, gain1_ref, bias1_ref, mine_ref, got_ref, bdown_ref, gain2_ref, grad_ref, pick_ref,
    dz2_ref, low_ref, sum_ref,
):
    h1 = normed_ref[...] * row_of(gain1_ref) + row_of(bias1_ref)
    branch = mine_ref[...].astype(f32) + got_ref[...].astype(f32) + row_of(bdown_ref)
    normed, inv_std = norm_stats(h1 + branch)
    used = jnp.sum(pick_ref[...].astype(f32), axis=1, keepdims=True)
    cot = jnp.where(used > 0.0, grad_ref[...].astype(f32), 0.0)
    dz2, g_gain, g_bias = norm_backward(cot, normed, inv_std, row_of(gain2_ref))
    dz2_ref[...] = dz2
    low = dz2.astype(bf16)
    low_ref[...] = low
    sum_ref[...] = jnp.concatenate(
        [col_sum(low.astype(f32)), g_gain, g_bias, jnp.zeros((5, h1.shape[1]), f32)], axis=0
    )


def norm_picked(normed, gain1, bias1, mine, got, b_down, gain2, grads, pick):
    picks, width = normed.shape
    return pl.pallas_call(
        norm_picked_kernel,
        out_shape=[
            jax.ShapeDtypeStruct((picks, width), f32),
            jax.ShapeDtypeStruct((picks, width), bf16),
            jax.ShapeDtypeStruct((8, width), f32),
        ],
        compiler_params=PARAMS,
        name="norm_picked",
    )(normed, gain1, bias1, mine, got, b_down, gain2, grads, pick)


def ffn_full_kernel(
    x_ref, ctx_ref, ctx2_ref, wo_ref, bo_ref, gain1_ref, bias1_ref, bdown_ref, gain2_ref, bias2_ref,
    bin_ref, bin2_ref, bin3_ref, win_ref, down_ref, win2_ref, down2_ref, win3_ref, down3_ref,
    out_ref, h1, low, total, win_here, down_here, win_sem, down_sem,
):
    rows, width = x_ref.shape
    tile = win_here.shape[2]
    parts = [(win_ref, down_ref, bin_ref, n * tile) for n in range(win_ref.shape[1] // tile)]
    parts += [(win2_ref, down2_ref, bin2_ref, 0), (win3_ref, down3_ref, bin3_ref, 0)]

    def copies(n):
        w_ref, d_ref, _, at = parts[n]
        return (
            pltpu.make_async_copy(w_ref.at[:, at : at + tile], win_here.at[n], win_sem.at[n]),
            pltpu.make_async_copy(d_ref.at[at : at + tile, :], down_here.at[n], down_sem.at[n]),
        )

    for n in range(len(parts)):
        for copy in copies(n):
            copy.start()
    attn = dot_nn(ctx_ref[...], wo_ref[: ctx_ref.shape[1]]) + dot_nn(
        ctx2_ref[...], wo_ref[ctx_ref.shape[1] :]
    )
    normed, _ = norm_stats(x_ref[...].astype(f32) + (attn + row_of(bo_ref)))
    value = normed * row_of(gain1_ref) + row_of(bias1_ref)
    h1[...] = value
    low[...] = value.astype(bf16)
    step = rows // 2
    for n in range(len(parts)):
        for copy in copies(n):
            copy.wait()
        bias = parts[n][2][:, parts[n][3] : parts[n][3] + tile]
        for at in range(0, rows, step):
            pre = dot_nn(low[at : at + step], win_here[n]) + bias
            part = dot_nn((pre * normal_cdf(pre)).astype(bf16), down_here[n])
            total[at : at + step] = part if n == 0 else total[at : at + step] + part
    normed, _ = norm_stats(h1[...] + (total[...] + row_of(bdown_ref)))
    out_ref[...] = (normed * row_of(gain2_ref) + row_of(bias2_ref)).astype(bf16)


def ffn_full(x, ctx, w_out, b_out, gain1, bias1, shards, b_down, gain2, bias2):
    rows, width = x.shape
    tile = shards[1][0].shape[1]
    count = shards[0][0].shape[1] // tile + 2
    held = [x, ctx[0], ctx[1], w_out, b_out, gain1, bias1, b_down, gain2, bias2]
    held += [shard[2] for shard in shards]
    moved = [value for shard in shards for value in shard[:2]]
    return pl.pallas_call(
        ffn_full_kernel,
        in_specs=[pl.BlockSpec(memory_space=pltpu.VMEM)] * len(held)
        + [pl.BlockSpec(memory_space=pl.ANY)] * len(moved),
        out_specs=pl.BlockSpec(memory_space=pltpu.VMEM),
        out_shape=jax.ShapeDtypeStruct((rows, width), bf16),
        scratch_shapes=[
            pltpu.VMEM((rows, width), f32), pltpu.VMEM((rows, width), bf16), pltpu.VMEM((rows, width), f32),
            pltpu.VMEM((count, width, tile), bf16), pltpu.VMEM((count, tile, width), bf16),
            pltpu.SemaphoreType.DMA((count,)), pltpu.SemaphoreType.DMA((count,)),
        ],
        compiler_params=PARAMS,
        name="ffn_full",
    )(*held, *moved)


def token_grads_kernel(pick_ref, dz1_ref, dq_ref, dk_ref, dv_ref, wq_ref, wk_ref, wv_ref, out_ref):
    sparse = dz1_ref[...] + dot_nt(dq_ref[...], wq_ref[...])
    upper = sparse.astype(bf16)
    lower = (sparse - upper.astype(f32)).astype(bf16)
    out_ref[...] = (
        dot_nt(dk_ref[...], wk_ref[...])
        + dot_nt(dv_ref[...], wv_ref[...])
        + dot_tn(pick_ref[...], upper)
        + dot_tn(pick_ref[...], lower)
    )


def token_grads(pick, dz1, dq, dk, dv, w_query, w_key, w_value):
    seq, width = dk.shape
    group = 2 * LANES
    whole = lambda value: pl.BlockSpec(value.shape, lambda n: (0, 0))
    col = lambda rows: pl.BlockSpec((rows, group), lambda n: (0, n))
    row = pl.BlockSpec((group, width), lambda n: (n, 0))
    return pl.pallas_call(
        token_grads_kernel,
        grid=(width // group,),
        in_specs=[whole(pick), col(dz1.shape[0]), whole(dq), whole(dk), whole(dv), row, row, row],
        out_specs=col(seq),
        out_shape=jax.ShapeDtypeStruct((seq, width), f32),
        compiler_params=PARAMS,
        name="token_grads",
    )(pick, dz1, dq, dk, dv, w_query, w_key, w_value)


def grads_kernel(
    half, planes, unit, me_ref, order_ref, relorder_ref, taker_ref,
    x_ref, rel_ref, xpick_ref, cpick_ref, dpos_ref,
    dq_ref, dk_ref, dv_ref, dattn_ref, dposk_ref, dposq_ref, wq_ref, wk_ref,
    early_ref, bin_ref, bin2_ref, *refs
):
    width = x_ref.shape[0]
    group = 2 * LANES
    dpos = refs[-1]

    def left(ref):
        starts = range(half * LANES, width, group)
        return jnp.concatenate([ref[at : at + LANES, :] for at in starts], axis=0)

    def put(at, value):
        for n in range(value.shape[0] // LANES):
            block = value[n * LANES : (n + 1) * LANES]
            if half:
                refs[0][at + n] = block.astype(bf16)
            else:
                block = (block + refs[0][at + n].astype(f32)).astype(bf16)
                refs[1][at + n] = block[: LANES // 2]
                refs[2][at + n] = block[LANES // 2 :]

    @pl.when(pl.program_id(0) == 0)
    def _():
        rows = order_rows(relorder_ref, me_ref, dpos_ref.shape[1])
        starts = range(half * LANES, rows.shape[0], group)
        rows = jnp.concatenate([rows[at : at + LANES] for at in starts], axis=0)
        for n in range(2):
            dpos[n] = dot_nn(rows, dpos_ref[n]).astype(bf16)

    count = width // group
    rel_left = left(rel_ref)
    x_left = left(x_ref)
    put(0, dot_nn(left(xpick_ref), dq_ref[...]) + dot_nn(rel_left, dposq_ref[0]))
    put(count, dot_nn(x_left, dk_ref[...]) + dot_nn(rel_left, dposk_ref[0]))
    put(2 * count, dot_nn(x_left, dv_ref[...]))
    put(3 * count, dot_nn(left(cpick_ref), dattn_ref[...]))
    put(4 * count, dot_nt(dpos[0], wk_ref[...]) + dot_nt(dpos[1], wq_ref[...]))

    total = lambda value: col_sum(value.astype(f32))
    values = jnp.concatenate(
        [
            total(dq_ref[...]) + total(dposq_ref[0]),
            total(dk_ref[...]) + total(dposk_ref[0]),
            total(dv_ref[...]),
            early_ref[:6],
            bin_ref[:1],
            bin2_ref[:1],
            jnp.zeros((5, group), f32),
        ],
        axis=0,
    )
    block = block_rows(order_ref[half * LANES : (half + 1) * LANES, :], me_ref)
    tok_place = jnp.where(block % me_ref[3] == me_ref[0] % me_ref[3], block // me_ref[3], -1)
    first = 4 * count + dpos.shape[1] // LANES
    row = lax.broadcasted_iota(jnp.int32, (LANES, 1), 0) % unit
    for n in range(first, planes):
        rows = slice((n - first) * unit, (n - first + 1) * unit)
        spread = lambda value: jnp.concatenate([value[rows]] * (LANES // unit), axis=0)
        taker = jnp.where(row + rows.start < VECTORS, block, tok_place)
        put(n, jnp.where(spread(taker_ref[...]) == taker, spread(values), 0.0))


def weight_grads(
    half, unit, me, order, rel_order, takers, x, rel, x_pick, c_pick, dpos, dq, dk, dv, dattn,
    w_query, w_key, early, bins, *got
):
    width, seq = x.shape
    group = 2 * LANES
    planes = 4 * (width // group) + dpos.shape[1] // group + 16 // unit
    whole = lambda value: pl.BlockSpec(value.shape, lambda n: (0,) * value.ndim)
    col = lambda value: pl.BlockSpec((value.shape[0], group), lambda n: (0, n))
    row = lambda value: pl.BlockSpec((group, value.shape[1]), lambda n: (n, 0))
    plane = lambda t: pl.BlockSpec((1, dpos.shape[1], group), lambda n: (t, 0, n))
    block = lambda rows: pl.BlockSpec((planes, rows, group), lambda n: (0, 0, n))
    shape = lambda rows: jax.ShapeDtypeStruct((planes, rows, width), bf16)
    rows = [LANES] if half else [LANES // 2] * 2
    return pl.pallas_call(
        functools.partial(grads_kernel, half, planes, unit),
        grid=(width // group,),
        in_specs=[
            pl.BlockSpec(memory_space=pltpu.SMEM), whole(order), whole(rel_order), col(takers),
            whole(x), whole(rel), whole(x_pick), whole(c_pick), whole(dpos),
            col(dq), col(dk), col(dv), col(dattn), plane(0), plane(1), row(w_query), row(w_key),
            col(early), col(bins), pl.BlockSpec((8, group), lambda n: (0, n + width // group)),
        ]
        + [block(LANES) for _ in got],
        out_specs=[block(count) for count in rows],
        out_shape=[shape(count) for count in rows],
        scratch_shapes=[pltpu.VMEM((2, dpos.shape[1] // 2, width), bf16)],
        compiler_params=PARAMS,
        name="weight_grads",
    )(
        me, order, rel_order, takers, x, rel, x_pick, c_pick, dpos, dq, dk, dv, dattn, dpos, dpos,
        w_query, w_key, early, bins, bins, *got
    )


def swap(values, axis, bit):
    size = lax.axis_size(axis)
    return lax.ppermute(values, axis, [(n, n ^ bit) for n in range(size)])


def after(values, *others):
    return lax.optimization_barrier((values, others))[0]


class Halving:
    def __init__(self, axes, core, near, size):
        rest = [1 << n for n in range(size.bit_length() - 1) if (1 << n) != core]
        near = [bit for bit in near if bit in rest]
        rest = [bit for bit in rest if bit not in near]
        turned = near[-1:] + near[:-1]
        self.axes, self.core, self.size = axes, core, size
        self.orders = [[core] + near + rest, [core] + turned + rest]
        self.steps = len(self.orders[0])
        self.me = lax.axis_index(axes)
        self.upper = (self.me // core) % 2

    def core_of(self, place):
        return (place // self.core) % 2

    def send(self, values, step):
        pairs = [(n, n ^ self.orders[self.core_of(n)][step]) for n in range(self.size)]
        return lax.ppermute(values, self.axes, pairs)

    def relative(self, upper):
        masks = []
        for place in range(self.size):
            bits = [(place >> (self.steps - 1 - step)) & 1 for step in range(self.steps)]
            order = self.orders[upper ^ bits[0]]
            mask = 0
            for step, bit in enumerate(bits):
                mask ^= bit * order[step]
            masks.append(mask)
        return np.array(masks, np.int32)

    def order(self, length, unit):
        spots = np.arange(length)
        group = self.size * unit
        place = spots % group // unit
        rows = [self.relative(upper)[place] for upper in range(2)]
        rows.append(spots // group * unit + spots % unit)
        return np.stack(rows).astype(np.int32)

    def matrix(self, length, unit):
        first, second, inner = self.order(length, unit)
        source = (self.me ^ jnp.where(self.upper == 0, first, second)) * (length // self.size) + inner
        spot = lax.broadcasted_iota(jnp.int32, (length, length), 0)
        return (spot == source[None, :]).astype(bf16)


def local(
    tokens, rel_ids, mask_pos, grad_vals, w_query, w_key, w_value, w_out, b_query, b_key,
    b_value, b_out, rel_table, ln1_gain, ln1_bias, w_in, b_in, w_down, b_down, ln2_gain, ln2_bias,
):
    assert rel_ids.shape[0] == 1
    seq, width = tokens.shape
    table_rows = rel_table.shape[0]
    hidden_cols = w_in.shape[1]
    pairs = width // LANES
    n_tok = lax.axis_size("tok")
    n_ffn = lax.axis_size("ffn")
    n_all = n_tok * n_ffn
    low = lambda value: value.astype(bf16)
    wide = lambda value: value.astype(f32)
    rel_ids, positions, grad_vals = rel_ids[0], mask_pos[0], grad_vals[0]

    over_all = Halving(("tok", "ffn"), n_ffn, [2 * n_ffn, 1, 4 * n_ffn], n_all)
    own, own_rel = width // n_all, table_rows // n_all
    unit = math.gcd(own, own_rel)
    group = n_all * unit
    over_tok = Halving("tok", 1, [2, 4], n_tok)
    pad = lambda value, count: np.pad(value, ((0, count - value.shape[0]), (0, 0)))
    order = jnp.asarray(pad(over_all.order(width, unit), LANES).T)
    rel_order = jnp.asarray(pad(over_all.order(table_rows, unit), LANES).T)
    spots = np.arange(width)
    takers = [spots // own] * VECTORS
    takers += [(spots + n * width) // (hidden_cols // n_tok) for n in range(hidden_cols // width)]
    takers = np.stack(takers).astype(np.int32)
    takers = jnp.asarray(np.pad(takers, ((0, 16 - takers.shape[0]), (0, 0)), constant_values=-2))
    me = jnp.stack([over_all.me, over_all.upper, jnp.int32(n_all), jnp.int32(n_ffn)])
    table_of = jnp.asarray(np.repeat(distance_rows(seq, table_rows)[:, None], LANES, 1))

    core = lax.axis_index("tok") % 2
    half_cols = hidden_cols // 2
    bias_row = b_in.reshape(1, hidden_cols)
    in_half = lax.dynamic_slice_in_dim(w_in, core * half_cols, half_cols, 1)
    down_half = lax.dynamic_slice_in_dim(w_down, core * half_cols, half_cols, 0)

    pick = low(positions[:, None] == lax.broadcasted_iota(jnp.int32, (positions.shape[0], seq), 1))
    x_pick = low(dot_nn(pick, tokens))
    q_pick = low(dot_nn(x_pick, w_query) + b_query)
    k = low(dot_nn(tokens, w_key) + b_key)
    v = low(dot_nn(tokens, w_value) + b_value)
    pos_query = low(dot_nn(rel_table, w_query) + b_query)
    pos_key = low(dot_nn(rel_table, w_key) + b_key)
    ctx_pick, probs, key_scores, words, words_pick, normed1, inv1, h1_mine = attend_picked(
        positions, rel_ids, q_pick, k, v, pos_query, pos_key, x_pick, w_out, b_out, ln1_gain, ln1_bias
    )

    h1_theirs = swap(h1_mine, "ffn", 1)
    bias_theirs = swap(bias_row, "ffn", 1)
    x_turned, x_pick_turned, c_pick_turned, rel_turned = turn_blocks(
        me, order, tokens, x_pick, ctx_pick, rel_table
    )
    h1_both = jnp.concatenate([h1_mine, after(h1_theirs, x_turned)], axis=0)
    count = h1_mine.shape[0]
    pre = dot_nn(h1_both, w_in) + b_in
    cdf = normal_cdf(pre)
    hidden = low(pre * cdf)
    slope = cdf + pre * (jnp.exp(-0.5 * pre * pre) * (1.0 / math.sqrt(2.0 * math.pi)))
    part = low(dot_nn(hidden, w_down))
    got = swap(part[count:], "ffn", 1)
    q = low(dot_nn(after(tokens, part), w_query) + b_query)
    tok_order = over_tok.matrix(width, width // n_tok)
    h1_left = low(dot_nn(h1_both, lax.optimization_barrier(tok_order)))
    in_half = after(in_half, part)
    got = after(got, q, h1_left, in_half)
    dz2, dffn, early = norm_picked(
        normed1, ln1_gain, ln1_bias, part[:count], got, b_down, ln2_gain, grad_vals, pick
    )
    down_half = after(down_half, dffn)
    dffn_both = jnp.concatenate([dffn, after(swap(dffn, "ffn", 1), down_half)], axis=0)
    dpre = low(dot_nt(dffn_both, w_down) * slope)
    dpart = low(dot_nt(dpre, w_in))
    dgot = swap(dpart[count:], "ffn", 1)

    def halves(values, axis):
        size = values.shape[axis] // 2
        cut = lambda at: lax.slice_in_dim(values, at, at + size, axis=axis)
        return cut(0), cut(size)

    add = lambda one, other: low(wide(one) + wide(other))

    def next_halves(kept, got, axis):
        return [add(one, other) for one, other in zip(halves(kept, axis), halves(got, axis))]

    dpre_later = after(dpre, dpart)
    dffn_left = low(dot_nn(after(dffn_both, dpart), tok_order))
    gb_in = dot_nn(jnp.ones((8, 2 * count), bf16), dpre_later)
    lefts, rights = (h1_left, dffn_left), (dpre_later, hidden)
    middle, quarter = width // 2, width // 4
    ffn_sent = [low(dot_tn(one[:, middle:], other)) for one, other in zip(lefts, rights)]
    dgot, ffn_sent = lax.optimization_barrier((dgot, ffn_sent))
    ffn_got = [over_tok.send(value, 0) for value in ffn_sent]
    far_in = swap(after(in_half, dgot, ffn_sent), "ffn", 1)

    def ffn_piece(at):
        return [
            low(dot_tn(one[:, at : at + quarter], other) + wide(value[at : at + quarter]))
            for one, other, value in zip(lefts, rights, ffn_got)
        ]

    ffn_sent = ffn_piece(quarter)
    ffn_kept = ffn_piece(0)
    ffn_got = [over_tok.send(value, 1) for value in ffn_sent]

    def ffn_next(step, kept, got):
        if step < over_tok.steps:
            pieces = [next_halves(one, other, 0) for one, other in zip(kept, got)]
            return [piece[0] for piece in pieces], [over_tok.send(piece[1], step) for piece in pieces]
        return [add(one, other) for one, other in zip(kept, got)], None

    dq, dk, dv, dpos, dz1, dattn, early = attend_back(
        table_of, words, words_pick, q_pick, k, v, probs, pos_query, pos_key,
        dz2, dpart[:count], after(dgot, in_half, ffn_sent, ffn_kept), normed1, inv1, ln1_gain, w_out, early,
    )
    far_in, ffn_got = after((far_in, ffn_got), dk)
    ffn_kept, ffn_got = ffn_next(2, ffn_kept, ffn_got)

    def grads(half, dk, *more):
        return weight_grads(
            half, unit, me, order, rel_order, takers,
            x_turned, rel_turned, x_pick_turned, c_pick_turned, dpos, dq, dk, dv, dattn,
            w_query, w_key, early, gb_in, *more,
        )

    (all_send,) = grads(1, after(dk, far_in, ffn_kept))
    near_in = swap(far_in, "tok", 1)
    far_down = swap(after(down_half, far_in), "ffn", 1)
    all_got = over_all.send(all_send, 0)
    grad_tokens = token_grads(pick, dz1, dq, after(dk, all_send), dv, w_query, w_key, w_value)
    all_kept, all_sent = grads(0, after(dk, grad_tokens), all_got)
    ffn_step = 3

    def attend(first, count, q):
        return attend_full(rel_ids, q, k, v, pos_key, key_scores, first, count)

    ctx = []
    for step in range(1, over_all.steps):
        all_got = over_all.send(all_sent, step)
        if step == 1:
            ctx.append(attend(0, FIRST_PAIRS, after(q, all_sent)))
            fill = ctx[-1]
        elif step == 2:
            ctx.append(attend(FIRST_PAIRS, pairs - FIRST_PAIRS, after(q, all_sent)))
            fill = ctx[-1]
        elif step == 3:
            near_down = swap(far_down, "tok", 1)
            biases = [
                lax.dynamic_slice_in_dim(bias_theirs, at * half_cols, half_cols, 1)
                for at in (core, 1 - core)
            ]
            shards = [
                (w_in, w_down, bias_row), (far_in, far_down, biases[0]), (near_in, near_down, biases[1])
            ]
            output = ffn_full(
                after(tokens, all_sent), ctx, w_out, b_out, ln1_gain, ln1_bias, shards,
                b_down, ln2_gain, ln2_bias,
            )
            fill = output
        if step <= 3:
            all_got = after(all_got, fill)
        if step <= 2 and ffn_step <= over_tok.steps:
            ffn_kept, ffn_got = ffn_next(ffn_step, ffn_kept, after(ffn_got, fill))
            all_got = after(all_got, ffn_kept)
            ffn_step += 1
        if step < over_all.steps - 1:
            all_kept, all_sent = next_halves(all_kept, all_got, 1)
        else:
            all_sums = add(all_kept, all_got)
    for step in range(ffn_step, over_tok.steps + 1):
        ffn_kept, ffn_got = ffn_next(step, ffn_kept, ffn_got)

    planes = 4 * (width // group) + table_rows // group
    vectors = wide(all_sums[planes:].reshape(16, width))
    all_sums = all_sums[:planes].reshape(planes * unit, width)
    s_w = [wide(all_sums[n * own : (n + 1) * own]) for n in range(4)]
    s_rel = wide(all_sums[4 * own :])
    s_vec = lax.dynamic_slice_in_dim(vectors[:VECTORS], over_all.me * own, own, 1)
    part = hidden_cols // n_tok
    bins = vectors[VECTORS : VECTORS + hidden_cols // width].reshape(1, hidden_cols)
    s_bin = lax.dynamic_slice_in_dim(bins, lax.axis_index("tok") * part, part, 1)
    return (
        output,
        grad_tokens,
        s_w[0],
        s_w[1],
        s_w[2],
        s_w[3],
        s_vec[0],
        s_vec[1],
        s_vec[2],
        s_vec[3],
        s_rel,
        s_vec[4],
        s_vec[5],
        wide(ffn_kept[0]),
        s_bin,
        jnp.transpose(wide(ffn_kept[1])),
        s_vec[6],
        s_vec[7],
        s_vec[8],
    )


def solution(mesh):
    every = ("tok", "ffn")
    placed = (
        P(every, None), P(every, None, None), P(every, None), P(every, None, None),
        P(), P(), P(), P(), P(), P(), P(), P(), P(), P(), P(),
        P(None, "ffn"), P("ffn"), P("ffn", None), P(), P(), P(),
    )
    given = (
        P(every, None), P(every, None),
        P(every, None), P(every, None), P(every, None), P(every, None),
        P(every), P(every), P(every), P(every),
        P(every, None), P(every), P(every),
        P("tok", "ffn"), P("ffn", "tok"), P("ffn", "tok"),
        P(every), P(every), P(every),
    )
    return jax.shard_map(local, mesh=mesh, in_specs=placed, out_specs=given, check_vma=False)
```

profile of v0, /device:TPU:0, one launch (start us, length us, event | category | flops | bytes accessed | tf_op | source)
XLA Modules:
  0.0 234.1 jit_solution(11800654759829051360)
XLA Ops:
  0.7 1.5 convolution_convert_fusion.5.x_ref.xpick_ref
  2.2 3.3 %add_convert_fusion.6.k_ref = bf16[512,768]{1,0:T(8,128)(2,1)} fusion(bf16[512,768]{1,0:T(8,128)(2,1)} %x_ref.2, bf16[768,768]{1,0:T(8,128)(2,1)} %wk_ref.5, f32[768]{0:T(1024)} %param.37), kind=kOutput, calls=%fused_computation.14 | convolution fusion | flops 604766208 | bytes 2755584 | tf_op jit(solution)/shard_map/dot_general | solution.py:27
  5.5 1.8 add_convert_fusion.4.pk_ref
  7.2 1.7 add_convert_fusion.3.pq_ref
  8.9 1.0 fusion.5.qc_ref
  10.1 1.7 add_convert_fusion.5.v_ref
  11.8 30.3 %attend_picked.1 = (bf16[80,768]{1,0:T(8,128)(2,1)}, bf16[12,80,512]{2,1,0:T(8,128)(2,1)}, f32[12,512,512]{2,1,0:T(8,128)}, s32[512,128]{1,0:T(8,128)}, s32[80,1...) custom-call(s32[80]{0:T(128)} %bitcast.98, s32[512,512]{1,0:T(8,128)} %bitcast.91, ...), custom_call_target="tpu_custom_call" | custom-call | tf_op jit(solution)/shard_map/attend_picked/pallas_call | solution.py:277
  42.1 3.0 %collective-permute-start = (bf16[80,768]{1,0:T(8,128)(2,1)}, bf16[80,768]{1,0:T(8,128)(2,1)}, u32[]{:S(2)}, u32[]{:S(2)}) collective-permute-start(bf16[80,768]{1,0:T(8,128)(2,1)} %get-tuple-element.84), channel_id=1, source_target_pairs={{0,1},{1,0},{2,3},{3,2},{4,5},{5,4},{6,7},{7,6},{8,9},{9,8},{10,11... | collective-permute-start | bytes 368648 | tf_op jit(solution)/shard_map/ppermute | solution.py:796
  45.1 0.7 fusion.10.pick_ref
  45.8 0.7 multiply_add_fusion
  46.5 1.4 fusion.2
  48.0 1.1 constant_dynamic-slice_fusion.5
  49.7 5.1 %turn_blocks.1 = (bf16[768,512]{1,0:T(8,128)(2,1)}, bf16[768,80]{1,0:T(8,128)(2,1)}, bf16[768,80]{1,0:T(8,128)(2,1)}, bf16[768,512]{1,0:T(8,128)(2,1)}) custom-call(s32[4]{0:T(128)} %pad_add_fusion.me_ref, s32[768,128]{1,0:T(8,128)} %constant.90.clone.order_ref, bf16[512,768]{1,0:T(8,128)(2,1)} %x_ref.2, bf16[80,768]{1,0:T(8,128)(2,1)} %copy-done.9, ...), custom_call_target="tpu_custom_call" | custom-call | tf_op jit(solution)/shard_map/turn_blocks/pallas_call | solution.py:558
  54.8 0.9 constant_dynamic-update-slice_fusion
  55.8 1.6 multiply_convert_fusion
  58.1 0.7 fusion.42
  58.9 1.7 add_convert_fusion.2.q_ref
  60.9 2.9 %collective-permute-done.1.got_ref = bf16[80,768]{1,0:T(8,128)(2,1)} collective-permute-done((bf16[80,768]{1,0:T(8,128)(2,1)S(1)}, bf16[80,768]{1,0:T(8,128)(2,1)}, u32[]{:S(2)}, u32[]{:S(2)}) %collective-permute-start.1) | collective-permute-done | bytes 122912 | tf_op jit(solution)/shard_map/ppermute | solution.py:796
  63.8 2.4 %norm_picked.1 = (f32[80,768]{1,0:T(8,128)}, bf16[80,768]{1,0:T(8,128)(2,1)}, f32[8,768]{1,0:T(8,128)}) custom-call(f32[80,768]{1,0:T(8,128)} %get-tuple-element.83.normed_ref, f32[768]{0:T(1024)} %gain1_ref.3, f32[768]{0:T(1024)} %bias1_ref.3, bf16[80,768]{1,0:T(8,128)(2,1)} %get-tuple-element.150.mine_ref, bf16[80,768]{1,0:T(8,128)(2,1)} %collective-permute-done.1.got_ref, ...), custom_call_target="tpu_custom_call" | custom-call | tf_op jit(solution)/shard_map/norm_picked/pallas_call | solution.py:590
  66.5 2.6 %constant_dynamic-slice_fusion.4 = bf16[768,768]{1,0:T(8,128)(2,1)} fusion(bf16[1536,768]{1,0:T(8,128)(2,1)} %down_ref.1, s32[]{:T(128)S(6)} %select_n.45), kind=kLoop, calls=%fused_computation.87 | loop fusion | bytes 2359300 | tf_op jit(solution)/shard_map/dynamic_slice | solution.py:884
  69.1 2.2 collective-permute-done.2
  71.3 2.2 fusion
  73.5 0.9 convolution_convert_fusion.3
  74.4 0.7 fusion.41
  75.9 0.6 fusion.3
  77.0 3.0 %collective-permute-done.3.got_ref = bf16[80,768]{1,0:T(8,128)(2,1)S(1)} collective-permute-done((bf16[80,768]{1,0:T(8,128)(2,1)S(1)}, bf16[80,768]{1,0:T(8,128)(2,1)S(1)}, u32[]{:S(2)}, u32[]{:S(2)}) %collective-permute-start.3) | collective-permute-done | bytes 122912 | tf_op jit(solution)/shard_map/ppermute | solution.py:796
  80.0 0.7 copy-done.20
  80.9 1.9 collective-permute-done.4
  82.8 1.2 add_convert_fusion.10
  84.1 1.5 collective-permute-start.7
  85.6 1.2 add_convert_fusion.9
  87.3 0.8 fusion.36.bin_ref.bin2_ref
  88.8 24.4 %attend_back.1 = (bf16[80,768]{1,0:T(8,128)(2,1)}, bf16[512,768]{1,0:T(8,128)(2,1)}, bf16[512,768]{1,0:T(8,128)(2,1)}, bf16[2,512,768]{2,1,0:T(8,128)(2,1)}, f32...) custom-call(s32[1024,128]{1,0:T(8,128)} %constant.93.clone.row_ref, ...), custom_call_target="tpu_custom_call" | custom-call | tf_op jit(solution)/shard_map/attend_back/pallas_call | solution.py:494
  113.3 1.6 add_convert_fusion.14
  114.9 1.9 add_convert_fusion.13
  116.8 11.4 %weight_grads.2 = bf16[16,128,768]{2,1,0:T(8,128)(2,1)} custom-call(s32[4]{0:T(128)} %pad_add_fusion.me_ref, s32[768,128]{1,0:T(8,128)} %constant.90.clone.order_ref, s32[512,128]{1,0:T(8,128)} %constant.91.clone.relorder_ref, s32[16,768]{1,0:T(8,128)} %constant.92.clone.taker_ref, bf16[768,512]{1,0:T(8,128)(2,1)} %get-tuple-element.76.x_ref, ...), custom_call_target="tpu_custom_call" | custom-call | tf_op jit(solution)/shard_map/weight_grads/pallas_call | solution.py:773
  128.2 5.9 %token_grads.1 = f32[512,768]{1,0:T(8,128)} custom-call(bf16[80,512]{1,0:T(8,128)(2,1)} %fusion.10.pick_ref, f32[80,768]{1,0:T(8,128)} %get-tuple-element.104.dz1_ref, bf16[80,768]{1,0:T(8,128)(2,1)} %get-tuple-element.102.dq_ref, bf16[512,768]{1,0:T(8,128)(2,1)} %get-tuple-element.114.dk_ref, bf16[512,768]{1,0:T(8,128)(2,1)} %get-tuple-element.110.dv_ref, ...), custom_call_target="tpu_custom_call" | custom-call | tf_op jit(solution)/shard_map/token_grads/pallas_call | solution.py:683
  134.2 1.6 copy-done.8
  135.8 11.9 %weight_grads.3 = (bf16[16,64,768]{2,1,0:T(8,128)(2,1)}, bf16[16,64,768]{2,1,0:T(8,128)(2,1)}) custom-call(s32[4]{0:T(128)} %pad_add_fusion.me_ref, s32[768,128]{1,0:T(8,128)} %constant.90.clone.order_ref, s32[512,128]{1,0:T(8,128)} %constant.91.clone.relorder_ref, s32[16,768]{1,0:T(8,128)} %constant.92.clone.taker_ref, ...), custom_call_target="tpu_custom_call" | custom-call | tf_op jit(solution)/shard_map/weight_grads/pallas_call | solution.py:773
  147.6 1.6 collective-permute-start.10
  149.2 1.6 collective-permute-start.11
  151.7 10.2 %attend_full.2.ctx_ref = bf16[512,256]{1,0:T(8,128)(2,1)} custom-call(s32[512,512]{1,0:T(8,128)} %bitcast.92, bf16[512,768]{1,0:T(8,128)(2,1)} %add_convert_fusion.2.q_ref, bf16[512,768]{1,0:T(8,128)(2,1)} %add_convert_fusion.6.k_ref, bf16[512,768]{1,0:T(8,128)(2,1)} %add_convert_fusion.5.v_ref, bf16[512,768]{1,0:T(8,128)(2,1)} %add_convert_fusion.4.pk_ref, ...), custom_call_target="tpu_custom_call" | custom-call | tf_op jit(solution)/shard_map/attend_full/pallas_call | solution.py:368
  161.9 3.6 %collective-permute-done.12 = bf16[96,1536]{1,0:T(8,128)(2,1)S(1)} collective-permute-done((bf16[96,1536]{1,0:T(8,128)(2,1)}, bf16[96,1536]{1,0:T(8,128)(2,1)S(1)}, u32[]{:S(2)}, u32[]{:S(2)}) %collective-permute-start.12) | collective-permute-done | bytes 294944 | tf_op jit(solution)/shard_map/ppermute | solution.py:820
  165.5 0.7 add_convert_fusion.23
  166.2 0.7 add_convert_fusion.22
  166.9 7.7 %collective-permute-done.10 = bf16[16,64,768]{2,1,0:T(8,128)(2,1)S(1)} collective-permute-done((bf16[16,64,768]{2,1,0:T(8,128)(2,1)}, bf16[16,64,768]{2,1,0:T(8,128)(2,1)S(1)}, u32[]{:S(2)}, u32[]{:S(2)}) %collective-permute-start.10) | collective-permute-done | bytes 1572896 | tf_op jit(solution)/shard_map/ppermute | solution.py:820
  174.7 1.5 add_convert_fusion
  176.5 2.7 %collective-permute-start.14 = (bf16[48,1536]{1,0:T(8,128)(2,1)}, bf16[48,1536]{1,0:T(8,128)(2,1)S(1)}, u32[]{:S(2)}, u32[]{:S(2)}) collective-permute-start(bf16[48,1536]{1,0:T(8,128)(2,1)} %get-tuple-element.145), channel_id=1, source_target_pairs={{0,16},{2,18},{4,20},{6,22},{8,24},{10,26},{12,28},{14,30},{16,0},... | collective-permute-start | bytes 442376 | tf_op jit(solution)/shard_map/ppermute | solution.py:820
  180.0 17.3 %attend_full.3.ctx2_ref = bf16[512,512]{1,0:T(8,128)(2,1)} custom-call(s32[512,512]{1,0:T(8,128)} %bitcast.93, bf16[512,768]{1,0:T(8,128)(2,1)} %add_convert_fusion.2.q_ref, bf16[512,768]{1,0:T(8,128)(2,1)} %add_convert_fusion.6.k_ref, bf16[512,768]{1,0:T(8,128)(2,1)} %add_convert_fusion.5.v_ref, bf16[512,768]{1,0:T(8,128)(2,1)} %add_convert_fusion.4.pk_ref, ...), custom_call_target="tpu_custom_call" | custom-call | tf_op jit(solution)/shard_map/attend_full/pallas_call | solution.py:368
  197.3 0.9 convert_bitcast_fusion
  198.2 1.3 add_convert_fusion.11
  199.5 1.2 collective-permute-start.20
  200.7 1.6 collective-permute-start.16
  202.3 2.2 collective-permute-done.16
  205.1 1.0 copy-done.13
  206.1 10.8 %ffn_full.1 = bf16[512,768]{1,0:T(8,128)(2,1)} custom-call(bf16[512,768]{1,0:T(8,128)(2,1)} %x_ref.2, bf16[512,256]{1,0:T(8,128)(2,1)} %attend_full.2.ctx_ref, bf16[512,512]{1,0:T(8,128)(2,1)} %attend_full.3.ctx2_ref, bf16[768,768]{1,0:T(8,128)(2,1)} %wo_ref.5, f32[768]{0:T(1024)} %bo_ref.3, f32[768]{0:T(1024)} %gain1_ref.3, f32[768]{0:T(1024)} %bias1_ref.3, ...), custom_call_target="tpu_custom_call" | custom-call | tf_op jit(solution)/shard_map/ffn_full/pallas_call | solution.py:649
  217.0 1.0 add_convert_fusion.18
  217.9 2.7 %collective-permute-start.21 = (bf16[16,8,768]{2,1,0:T(8,128)(2,1)S(1)}, bf16[16,8,768]{2,1,0:T(8,128)(2,1)S(1)}, u32[]{:S(2)}, u32[]{:S(2)}) collective-permute-start(bf16[16,8,768]{2,1,0:T(8,128)(2,1)S(1)} %add_convert_fusion.18), channel_id=1, source_target_pairs={{0,16},{1,17},{2,18},{3,19},{4,20},{5,21},{6,22},{7,23},{8,24},{9,... | collective-permute-start | bytes 589832 | tf_op jit(solution)/shard_map/ppermute | solution.py:820
  220.6 9.7 %collective-permute-done.21 = bf16[16,8,768]{2,1,0:T(8,128)(2,1)S(1)} collective-permute-done((bf16[16,8,768]{2,1,0:T(8,128)(2,1)S(1)}, bf16[16,8,768]{2,1,0:T(8,128)(2,1)S(1)}, u32[]{:S(2)}, u32[]{:S(2)}) %collective-permute-start.21) | collective-permute-done | bytes 196640 | tf_op jit(solution)/shard_map/ppermute | solution.py:820
  230.4 1.0 add_convert_fusion.17
  231.4 0.7 fusion.30
  232.1 0.6 fusion.34
  232.7 0.6 constant_dynamic-slice_fusion.1
  233.3 0.6 dynamic-slice_bitcast_fusion
  (97 shorter events, 8.0 us)
Async XLA Ops:
  2.1 6.8 %copy-start.9 = (bf16[80,768]{1,0:T(8,128)(2,1)}, bf16[80,768]{1,0:T(8,128)(2,1)S(1)}, u32[]{:S(2)}) copy-start(bf16[80,768]{1,0:T(8,128)(2,1)S(1)} %convolution_convert_fusion.5.x_ref.xpick_ref) | copy-start | bytes 368644
  2.1 3.3 %copy-start.4 = (bf16[768,768]{1,0:T(8,128)(2,1)S(1)}, bf16[768,768]{1,0:T(8,128)(2,1)}, u32[]{:S(2)}) copy-start(bf16[768,768]{1,0:T(8,128)(2,1)} %wk_ref.5) | copy-start | bytes 3538948
  2.1 3.3 %copy-start.18 = (bf16[512,768]{1,0:T(8,128)(2,1)S(1)}, bf16[512,768]{1,0:T(8,128)(2,1)}, u32[]{:S(2)}) copy-start(bf16[512,768]{1,0:T(8,128)(2,1)} %rel_ref.1) | copy-start | bytes 2359300
  2.1 3.3 %copy-start.27 = (f32[768]{0:T(1024)S(1)}, f32[768]{0:T(1024)}, u32[]{:S(2)}) copy-start(f32[768]{0:T(1024)} %param.37) | copy-start | bytes 9220
  5.5 1.8 copy-start.1
  5.5 1.8 copy-start.25
  7.2 2.7 %copy-start.15 = (bf16[768,768]{1,0:T(8,128)(2,1)S(1)}, bf16[768,768]{1,0:T(8,128)(2,1)}, u32[]{:S(2)}) copy-start(bf16[768,768]{1,0:T(8,128)(2,1)} %wv_ref.1) | copy-start | bytes 3538948
  8.9 1.1 copy-start.5
  8.9 1.1 copy-start.28
  11.8 33.3 %copy-start.24 = (s32[1,80]{1,0:T(1,128)S(1)}, s32[1,80]{1,0:T(1,128)}, u32[]{:S(2)}) copy-start(s32[1,80]{1,0:T(1,128)} %param.30) | copy-start | bytes 964
  11.8 34.0 %copy-start.26 = (s32[768]{0:T(1024)S(1)}, s32[768]{0:T(1024)}, u32[]{:S(2)}) copy-start(s32[768]{0:T(1024)} %constant.96.clone) | copy-start | bytes 9220
  11.8 36.2 %copy-start = (bf16[768,1536]{1,0:T(8,128)(2,1)S(1)}, bf16[768,1536]{1,0:T(8,128)(2,1)}, u32[]{:S(2)}) copy-start(bf16[768,1536]{1,0:T(8,128)(2,1)} %win_ref.1) | copy-start | bytes 7077892
  42.1 12.7 %collective-permute-start = (bf16[80,768]{1,0:T(8,128)(2,1)}, bf16[80,768]{1,0:T(8,128)(2,1)}, u32[]{:S(2)}, u32[]{:S(2)}) collective-permute-start(bf16[80,768]{1,0:T(8,128)(2,1)} %get-tuple-element.84), channel_id=1, source_target_pairs={{0,1},{1,0},{2,3},{3,2},{4,5},{5,4},{6,7},{7,6},{8,9},{9,8},{10,11... | collective-permute-start | bytes 368648 | tf_op jit(solution)/shard_map/ppermute | solution.py:796
  49.1 5.7 %copy-start.19 = (bf16[80,768]{1,0:T(8,128)(2,1)S(1)}, bf16[80,768]{1,0:T(8,128)(2,1)}, u32[]{:S(2)}) copy-start(bf16[80,768]{1,0:T(8,128)(2,1)} %get-tuple-element.84) | copy-start | bytes 368644
  49.6 6.1 %copy-start.22 = (f32[1536]{0:T(1024)S(1)}, f32[1536]{0:T(1024)}, u32[]{:S(2)}) copy-start(f32[1536]{0:T(1024)} %param.44) | copy-start | bytes 18436
  55.7 1.8 copy-start.2
  57.6 1.3 copy-start.6
  58.8 1.8 copy-start.7
  58.8 5.0 %collective-permute-start.1 = (bf16[80,768]{1,0:T(8,128)(2,1)S(1)}, bf16[80,768]{1,0:T(8,128)(2,1)}, u32[]{:S(2)}, u32[]{:S(2)}) collective-permute-start(bf16[80,768]{1,0:T(8,128)(2,1)S(1)} %get-tuple-element.149), channel_id=1, source_target_pairs={{0,1},{1,0},{2,3},{3,2},{4,5},{5,4},{6,7},{7,6},{8,9},{9,8},{10,11... | collective-permute-start | bytes 368648 | tf_op jit(solution)/shard_map/ppermute | solution.py:796
  60.9 14.5 %copy-start.16 = (bf16[160,768]{1,0:T(8,128)(2,1)}, bf16[160,768]{1,0:T(8,128)(2,1)S(1)}, u32[]{:S(2)}) copy-start(bf16[160,768]{1,0:T(8,128)(2,1)S(1)} %convolution_convert_fusion.2) | copy-start | bytes 737284
  66.2 2.9 %copy-start.21 = (bf16[80,768]{1,0:T(8,128)(2,1)S(1)}, bf16[80,768]{1,0:T(8,128)(2,1)}, u32[]{:S(2)}) copy-start(bf16[80,768]{1,0:T(8,128)(2,1)} %get-tuple-element.90) | copy-start | bytes 368644
  66.2 5.2 %copy-start.3 = (bf16[1536,768]{1,0:T(8,128)(2,1)S(1)}, bf16[1536,768]{1,0:T(8,128)(2,1)}, u32[]{:S(2)}) copy-start(bf16[1536,768]{1,0:T(8,128)(2,1)} %down_ref.1) | copy-start | bytes 7077892
  66.2 5.1 %collective-permute-start.2 = (bf16[80,768]{1,0:T(8,128)(2,1)}, bf16[80,768]{1,0:T(8,128)(2,1)S(1)}, u32[]{:S(2)}, u32[]{:S(2)}) collective-permute-start(bf16[80,768]{1,0:T(8,128)(2,1)} %get-tuple-element.90), channel_id=1, source_target_pairs={{0,1},{1,0},{2,3},{3,2},{4,5},{5,4},{6,7},{7,6},{8,9},{9,8},{10,11... | collective-permute-start | bytes 368648 | tf_op jit(solution)/shard_map/ppermute | solution.py:796
  75.1 4.9 %collective-permute-start.3 = (bf16[80,768]{1,0:T(8,128)(2,1)S(1)}, bf16[80,768]{1,0:T(8,128)(2,1)S(1)}, u32[]{:S(2)}, u32[]{:S(2)}) collective-permute-start(bf16[80,768]{1,0:T(8,128)(2,1)S(1)} %get-tuple-element.147), channel_id=1, source_target_pairs={{0,1},{1,0},{2,3},{3,2},{4,5},{5,4},{6,7},{7,6},{8,9},{9,8},{10,11... | collective-permute-start | bytes 368648 | tf_op jit(solution)/shard_map/ppermute | solution.py:796
  76.5 4.2 %copy-start.14 = (bf16[768,768]{1,0:T(8,128)(2,1)S(1)}, bf16[768,768]{1,0:T(8,128)(2,1)}, u32[]{:S(2)}) copy-start(bf16[768,768]{1,0:T(8,128)(2,1)} %constant_dynamic-slice_fusion.5) | copy-start | bytes 3538948
  76.5 6.3 %copy-start.17 = (bf16[160,768]{1,0:T(8,128)(2,1)S(1)}, bf16[160,768]{1,0:T(8,128)(2,1)}, u32[]{:S(2)}) copy-start(bf16[160,768]{1,0:T(8,128)(2,1)} %copy-done.16) | copy-start | bytes 737284
  80.0 0.7 copy-start.20
  80.0 2.8 %collective-permute-start.4 = (bf16[384,1536]{1,0:T(8,128)(2,1)S(1)}, bf16[384,1536]{1,0:T(8,128)(2,1)S(1)}, u32[]{:S(2)}, u32[]{:S(2)}) collective-permute-start(bf16[384,1536]{1,0:T(8,128)(2,1)S(1)} %convolution_convert_fusion.1), channel_id=1, source_target_pairs={{0,2},{2,0},{4,6},{6,4},{8,10},{10,8},{12,14},{14,12},{16,18},{18,... | collective-permute-start | bytes 3538952 | tf_op jit(solution)/shard_map/ppermute | solution.py:820
  80.7 4.9 %collective-permute-start.5 = (bf16[384,1536]{1,0:T(8,128)(2,1)S(1)}, bf16[384,1536]{1,0:T(8,128)(2,1)S(1)}, u32[]{:S(2)}, u32[]{:S(2)}) collective-permute-start(bf16[384,1536]{1,0:T(8,128)(2,1)S(1)} %convolution_convert_fusion), channel_id=1, source_target_pairs={{0,2},{2,0},{4,6},{6,4},{8,10},{10,8},{12,14},{14,12},{16,18},{18,... | collective-permute-start | bytes 3538952 | tf_op jit(solution)/shard_map/ppermute | solution.py:820
  80.7 32.6 %collective-permute-start.6 = (bf16[768,768]{1,0:T(8,128)(2,1)S(1)}, bf16[768,768]{1,0:T(8,128)(2,1)S(1)}, u32[]{:S(2)}, u32[]{:S(2)}) collective-permute-start(bf16[768,768]{1,0:T(8,128)(2,1)S(1)} %copy-done.14), channel_id=1, source_target_pairs={{0,1},{1,0},{2,3},{3,2},{4,5},{5,4},{6,7},{7,6},{8,9},{9,8},{10,11... | collective-permute-start | bytes 3538952 | tf_op jit(solution)/shard_map/ppermute | solution.py:796
  84.1 29.2 %collective-permute-start.7 = (bf16[192,1536]{1,0:T(8,128)(2,1)}, bf16[192,1536]{1,0:T(8,128)(2,1)}, u32[]{:S(2)}, u32[]{:S(2)}) collective-permute-start(bf16[192,1536]{1,0:T(8,128)(2,1)} %add_convert_fusion.10), channel_id=1, source_target_pairs={{0,4},{2,10},{4,0},{6,14},{8,12},{10,2},{12,8},{14,6},{16,20},{18,... | collective-permute-start | bytes 1769480 | tf_op jit(solution)/shard_map/ppermute | solution.py:820
  86.8 26.4 %collective-permute-start.8 = (bf16[192,1536]{1,0:T(8,128)(2,1)}, bf16[192,1536]{1,0:T(8,128)(2,1)}, u32[]{:S(2)}, u32[]{:S(2)}) collective-permute-start(bf16[192,1536]{1,0:T(8,128)(2,1)} %add_convert_fusion.9), channel_id=1, source_target_pairs={{0,4},{2,10},{4,0},{6,14},{8,12},{10,2},{12,8},{14,6},{16,20},{18,... | collective-permute-start | bytes 1769480 | tf_op jit(solution)/shard_map/ppermute | solution.py:820
  113.2 3.5 %copy-start.11 = (bf16[768,768]{1,0:T(8,128)(2,1)}, bf16[768,768]{1,0:T(8,128)(2,1)S(1)}, u32[]{:S(2)}) copy-start(bf16[768,768]{1,0:T(8,128)(2,1)S(1)} %collective-permute-done.6.win2_ref) | copy-start | bytes 3538948
  128.1 6.0 %collective-permute-start.9 = (bf16[16,128,768]{2,1,0:T(8,128)(2,1)}, bf16[16,128,768]{2,1,0:T(8,128)(2,1)S(1)}, u32[]{:S(2)}, u32[]{:S(2)}) collective-permute-start(bf16[16,128,768]{2,1,0:T(8,128)(2,1)} %weight_grads.2), channel_id=1, source_target_pairs={{0,2},{1,3},{2,0},{3,1},{4,6},{5,7},{6,4},{7,5},{8,10},{9,11},{10,... | collective-permute-start | bytes 9437192 | tf_op jit(solution)/shard_map/ppermute | solution.py:820
  134.2 1.6 copy-start.8
  147.6 27.0 %collective-permute-start.10 = (bf16[16,64,768]{2,1,0:T(8,128)(2,1)}, bf16[16,64,768]{2,1,0:T(8,128)(2,1)S(1)}, u32[]{:S(2)}, u32[]{:S(2)}) collective-permute-start(bf16[16,64,768]{2,1,0:T(8,128)(2,1)} %get-tuple-element.116), channel_id=1, source_target_pairs={{0,4},{1,5},{2,10},{3,11},{4,0},{5,1},{6,14},{7,15},{8,12},{9,13},... | collective-permute-start | bytes 4718600 | tf_op jit(solution)/shard_map/ppermute | solution.py:820
  149.2 12.7 %collective-permute-start.11 = (bf16[96,1536]{1,0:T(8,128)(2,1)S(1)}, bf16[96,1536]{1,0:T(8,128)(2,1)S(1)}, u32[]{:S(2)}, u32[]{:S(2)}) collective-permute-start(bf16[96,1536]{1,0:T(8,128)(2,1)S(1)} %get-tuple-element.141), channel_id=1, source_target_pairs={{0,8},{2,6},{4,12},{6,2},{8,0},{10,14},{12,4},{14,10},{16,24},{18,... | collective-permute-start | bytes 884744 | tf_op jit(solution)/shard_map/ppermute | solution.py:820
  150.8 14.7 %collective-permute-start.12 = (bf16[96,1536]{1,0:T(8,128)(2,1)}, bf16[96,1536]{1,0:T(8,128)(2,1)S(1)}, u32[]{:S(2)}, u32[]{:S(2)}) collective-permute-start(bf16[96,1536]{1,0:T(8,128)(2,1)} %get-tuple-element.139), channel_id=1, source_target_pairs={{0,8},{2,6},{4,12},{6,2},{8,0},{10,14},{12,4},{14,10},{16,24},{18,... | collective-permute-start | bytes 884744 | tf_op jit(solution)/shard_map/ppermute | solution.py:820
  151.2 28.2 %collective-permute-start.17 = (bf16[768,768]{1,0:T(8,128)(2,1)}, bf16[768,768]{1,0:T(8,128)(2,1)}, u32[]{:S(2)}, u32[]{:S(2)}) collective-permute-start(bf16[768,768]{1,0:T(8,128)(2,1)} %constant_dynamic-slice_fusion.4), channel_id=1, source_target_pairs={{0,1},{1,0},{2,3},{3,2},{4,5},{5,4},{6,7},{7,6},{8,9},{9,8},{10,11... | collective-permute-start | bytes 3538952 | tf_op jit(solution)/shard_map/ppermute | solution.py:796
  161.9 12.8 %copy-start.10 = (bf16[16,64,768]{2,1,0:T(8,128)(2,1)S(1)}, bf16[16,64,768]{2,1,0:T(8,128)(2,1)}, u32[]{:S(2)}) copy-start(bf16[16,64,768]{2,1,0:T(8,128)(2,1)} %get-tuple-element.115) | copy-start | bytes 4718596
  174.7 4.8 %copy-start.12 = (bf16[768,768]{1,0:T(8,128)(2,1)S(1)}, bf16[768,768]{1,0:T(8,128)(2,1)}, u32[]{:S(2)}) copy-start(bf16[768,768]{1,0:T(8,128)(2,1)} %copy-done.11) | copy-start | bytes 3538948
  176.1 22.1 %collective-permute-start.13 = (bf16[16,32,768]{2,1,0:T(8,128)(2,1)}, bf16[16,32,768]{2,1,0:T(8,128)(2,1)}, u32[]{:S(2)}, u32[]{:S(2)}) collective-permute-start(bf16[16,32,768]{2,1,0:T(8,128)(2,1)} %get-tuple-element.135), channel_id=1, source_target_pairs={{0,1},{1,0},{2,6},{3,7},{4,5},{5,4},{6,2},{7,3},{8,9},{9,8},{10,14... | collective-permute-start | bytes 2359304 | tf_op jit(solution)/shard_map/ppermute | solution.py:820
  176.5 20.8 %collective-permute-start.14 = (bf16[48,1536]{1,0:T(8,128)(2,1)}, bf16[48,1536]{1,0:T(8,128)(2,1)S(1)}, u32[]{:S(2)}, u32[]{:S(2)}) collective-permute-start(bf16[48,1536]{1,0:T(8,128)(2,1)} %get-tuple-element.145), channel_id=1, source_target_pairs={{0,16},{2,18},{4,20},{6,22},{8,24},{10,26},{12,28},{14,30},{16,0},... | collective-permute-start | bytes 442376 | tf_op jit(solution)/shard_map/ppermute | solution.py:820
  179.2 18.1 %collective-permute-start.15 = (bf16[48,1536]{1,0:T(8,128)(2,1)}, bf16[48,1536]{1,0:T(8,128)(2,1)S(1)}, u32[]{:S(2)}, u32[]{:S(2)}) collective-permute-start(bf16[48,1536]{1,0:T(8,128)(2,1)} %get-tuple-element.143), channel_id=1, source_target_pairs={{0,16},{2,18},{4,20},{6,22},{8,24},{10,26},{12,28},{14,30},{16,0},... | collective-permute-start | bytes 442376 | tf_op jit(solution)/shard_map/ppermute | solution.py:820
  179.5 25.6 %collective-permute-start.18 = (bf16[768,768]{1,0:T(8,128)(2,1)S(1)}, bf16[768,768]{1,0:T(8,128)(2,1)S(1)}, u32[]{:S(2)}, u32[]{:S(2)}) collective-permute-start(bf16[768,768]{1,0:T(8,128)(2,1)S(1)} %copy-done.12), channel_id=1, source_target_pairs={{0,2},{2,0},{4,6},{6,4},{8,10},{10,8},{12,14},{14,12},{16,18},{18,... | collective-permute-start | bytes 3538952 | tf_op jit(solution)/shard_map/ppermute | solution.py:796
  179.5 25.6 %collective-permute-start.19 = (bf16[768,768]{1,0:T(8,128)(2,1)}, bf16[768,768]{1,0:T(8,128)(2,1)}, u32[]{:S(2)}, u32[]{:S(2)}) collective-permute-start(bf16[768,768]{1,0:T(8,128)(2,1)} %collective-permute-done.17.down2_ref), channel_id=1, source_target_pairs={{0,2},{2,0},{4,6},{6,4},{8,10},{10,8},{12,14},{14,12},{16,18},{18,... | collective-permute-start | bytes 3538952 | tf_op jit(solution)/shard_map/ppermute | solution.py:796
  199.5 17.4 %collective-permute-start.20 = (bf16[16,16,768]{2,1,0:T(8,128)(2,1)S(1)}, bf16[16,16,768]{2,1,0:T(8,128)(2,1)}, u32[]{:S(2)}, u32[]{:S(2)}) collective-permute-start(bf16[16,16,768]{2,1,0:T(8,128)(2,1)S(1)} %get-tuple-element.138), channel_id=1, source_target_pairs={{0,8},{1,9},{2,3},{3,2},{4,12},{5,13},{6,7},{7,6},{8,0},{9,1},{10,... | collective-permute-start | bytes 1179656 | tf_op jit(solution)/shard_map/ppermute | solution.py:820
  200.7 4.4 %copy-start.23 = (f32[1,1536]{1,0:T(1,128)}, f32[1,1536]{1,0:T(1,128)S(1)}, u32[]{:S(2)}) copy-start(f32[1,1536]{1,0:T(1,128)S(1)} %broadcast_in_dim.5.bin_ref) | copy-start | bytes 18436
  200.7 3.8 %collective-permute-start.16 = (f32[1,1536]{1,0:T(1,128)S(1)}, f32[1,1536]{1,0:T(1,128)S(1)}, u32[]{:S(2)}, u32[]{:S(2)}) collective-permute-start(f32[1,1536]{1,0:T(1,128)S(1)} %broadcast_in_dim.5.bin_ref), channel_id=1, source_target_pairs={{0,1},{1,0},{2,3},{3,2},{4,5},{5,4},{6,7},{7,6},{8,9},{9,8},{10,11... | collective-permute-start | bytes 18440 | tf_op jit(solution)/shard_map/ppermute | solution.py:796
  205.1 1.0 copy-start.13
  217.9 12.4 %collective-permute-start.21 = (bf16[16,8,768]{2,1,0:T(8,128)(2,1)S(1)}, bf16[16,8,768]{2,1,0:T(8,128)(2,1)S(1)}, u32[]{:S(2)}, u32[]{:S(2)}) collective-permute-start(bf16[16,8,768]{2,1,0:T(8,128)(2,1)S(1)} %add_convert_fusion.18), channel_id=1, source_target_pairs={{0,16},{1,17},{2,18},{3,19},{4,20},{5,21},{6,22},{7,23},{8,24},{9,... | collective-permute-start | bytes 589832 | tf_op jit(solution)/shard_map/ppermute | solution.py:820
where the time goes:
time: 238 us; the launch traced here: 234 us
  Pallas kernels  130 us (55%)
  waiting for transfers between devices  33.2 us (14%)
  matrix products  23.7 us (10%)
  starting transfers between devices  19.5 us (8%)
  other arithmetic  15.4 us (6%)
  local copies, waits for them, and re-layouts  11.6 us (5%)
    pallas_call x1, Pallas kernels, attend_picked(): pl.pallas_call(picked_kernel, grid=(pairs,), in_specs=[pl.BlockSpec(memor...  30.3 us
    pallas_call x2, Pallas kernels, attend_full(): pl.pallas_call(full_kernel, grid=(pairs // per,), in_specs=[pl.BlockSpec(...  27.5 us
    pallas_call x1, Pallas kernels, attend_back(): pl.pallas_call(back_kernel, grid=(pairs,), in_specs=[whole(table_of), who...  24.4 us
    pallas_call x2, Pallas kernels, weight_grads(): pl.pallas_call(functools.partial(grads_kernel, half, planes, unit), grid=...  23.2 us
    ppermute x13, waiting for transfers between devices, send(): return lax.ppermute(values, self.axes, pairs)  23 us
    dot_general x12, matrix products, dot_nn(): lax.dot_general(first_op, second_op, (((1,), (0,)), ((), ())), preferred_...  16.4 us
    ppermute x13, starting transfers between devices, send(): return lax.ppermute(values, self.axes, pairs)  12.9 us
    pallas_call x1, Pallas kernels, ffn_full(): pl.pallas_call(ffn_full_kernel, in_specs=[pl.BlockSpec(memory_space=pltpu...  10.8 us
  transfers between devices with their start and end apart: 22, of which 8 were waited for; matrix products, arithmetic and copies ran while one was open for 9% of the time, Pallas kernels for 32%

commit v1 on v0

--- a/solution.py
+++ b/solution.py
@@ -15,7 +15,7 @@
 HALF = 64
 ROWS = 32
 AT_ONCE = 2
-FIRST_PAIRS = 2
+FIRST_PAIRS = 4
 VECTORS = 9
 norm_eps = 1e-07
 bf16 = jnp.bfloat16
@@ -532,9 +532,9 @@
 
 
 def turn_kernel(
-    me_ref, order_ref, x_ref, xpick_ref, cpick_ref, rel_ref, x_out, xpick_out, cpick_out, rel_out
+    n_all, me_ref, order_ref, x_ref, xpick_ref, cpick_ref, rel_ref, x_out, xpick_out, cpick_out, rel_out
 ):
-    picked = order_rows(order_ref, me_ref, x_ref.shape[1])
+    picked = order_rows(order_ref, me_ref, x_ref.shape[1], n_all)
     for ref, out in ((x_ref, x_out), (xpick_ref, xpick_out), (cpick_ref, cpick_out), (rel_ref, rel_out)):
         out[...] = dot_nt(picked, ref[...]).astype(bf16)
 
@@ -543,20 +543,20 @@
     return me_ref[0] ^ jnp.where(me_ref[1] == 0, ref[:, 0:1], ref[:, 1:2])
 
 
-def order_rows(ref, me_ref, length):
-    source = block_rows(ref, me_ref) * (length // me_ref[2]) + ref[:, 2:3]
+def order_rows(ref, me_ref, length, n_all):
+    source = block_rows(ref, me_ref) * (length // n_all) + ref[:, 2:3]
     spot = lax.broadcasted_iota(jnp.int32, (ref.shape[0], length), 1)
     return (spot == source).astype(f32).astype(bf16)
 
 
-def turn_blocks(me, order, x, x_pick, ctx_pick, rel_table):
+def turn_blocks(n_all, me, order, x, x_pick, ctx_pick, rel_table):
     width = x.shape[1]
     group = 2 * LANES
     whole = lambda value: pl.BlockSpec(value.shape, lambda n: (0, 0))
     row = lambda count: pl.BlockSpec((group, count), lambda n: (n, 0))
     given = [x, x_pick, ctx_pick, rel_table]
     return pl.pallas_call(
-        turn_kernel,
+        functools.partial(turn_kernel, n_all),
         grid=(width // group,),
         in_specs=[pl.BlockSpec(memory_space=pltpu.SMEM), row(LANES)]
         + [whole(value) for value in given],
@@ -692,44 +692,31 @@
 
 
 def grads_kernel(
-    half, planes, unit, me_ref, order_ref, relorder_ref, taker_ref,
+    n_all, n_ffn, unit, me_ref, order_ref, relorder_ref, taker_ref,
     x_ref, rel_ref, xpick_ref, cpick_ref, dpos_ref,
     dq_ref, dk_ref, dv_ref, dattn_ref, dposk_ref, dposq_ref, wq_ref, wk_ref,
-    early_ref, bin_ref, bin2_ref, *refs
+    early_ref, bin_ref, bin2_ref, kept_ref, sent_ref, dpos,
 ):
     width = x_ref.shape[0]
     group = 2 * LANES
-    dpos = refs[-1]
-
-    def left(ref):
-        starts = range(half * LANES, width, group)
-        return jnp.concatenate([ref[at : at + LANES, :] for at in starts], axis=0)
 
     def put(at, value):
-        for n in range(value.shape[0] // LANES):
-            block = value[n * LANES : (n + 1) * LANES]
-            if half:
-                refs[0][at + n] = block.astype(bf16)
-            else:
-                block = (block + refs[0][at + n].astype(f32)).astype(bf16)
-                refs[1][at + n] = block[: LANES // 2]
-                refs[2][at + n] = block[LANES // 2 :]
+        value = value.astype(bf16)
+        for n in range(value.shape[0] // group):
+            kept_ref[at + n] = value[n * group : n * group + LANES]
+            sent_ref[at + n] = value[n * group + LANES : (n + 1) * group]
 
     @pl.when(pl.program_id(0) == 0)
     def _():
-        rows = order_rows(relorder_ref, me_ref, dpos_ref.shape[1])
-        starts = range(half * LANES, rows.shape[0], group)
-        rows = jnp.concatenate([rows[at : at + LANES] for at in starts], axis=0)
+        rows = order_rows(relorder_ref, me_ref, dpos_ref.shape[1], n_all)
         for n in range(2):
             dpos[n] = dot_nn(rows, dpos_ref[n]).astype(bf16)
 
     count = width // group
-    rel_left = left(rel_ref)
-    x_left = left(x_ref)
-    put(0, dot_nn(left(xpick_ref), dq_ref[...]) + dot_nn(rel_left, dposq_ref[0]))
-    put(count, dot_nn(x_left, dk_ref[...]) + dot_nn(rel_left, dposk_ref[0]))
-    put(2 * count, dot_nn(x_left, dv_ref[...]))
-    put(3 * count, dot_nn(left(cpick_ref), dattn_ref[...]))
+    put(0, dot_nn(xpick_ref[...], dq_ref[...]) + dot_nn(rel_ref[...], dposq_ref[0]))
+    put(count, dot_nn(x_ref[...], dk_ref[...]) + dot_nn(rel_ref[...], dposk_ref[0]))
+    put(2 * count, dot_nn(x_ref[...], dv_ref[...]))
+    put(3 * count, dot_nn(cpick_ref[...], dattn_ref[...]))
     put(4 * count, dot_nt(dpos[0], wk_ref[...]) + dot_nt(dpos[1], wq_ref[...]))
 
     total = lambda value: col_sum(value.astype(f32))
@@ -745,20 +732,21 @@
         ],
         axis=0,
     )
-    block = block_rows(order_ref[half * LANES : (half + 1) * LANES, :], me_ref)
-    tok_place = jnp.where(block % me_ref[3] == me_ref[0] % me_ref[3], block // me_ref[3], -1)
-    first = 4 * count + dpos.shape[1] // LANES
-    row = lax.broadcasted_iota(jnp.int32, (LANES, 1), 0) % unit
-    for n in range(first, planes):
-        rows = slice((n - first) * unit, (n - first + 1) * unit)
-        spread = lambda value: jnp.concatenate([value[rows]] * (LANES // unit), axis=0)
-        taker = jnp.where(row + rows.start < VECTORS, block, tok_place)
-        put(n, jnp.where(spread(taker_ref[...]) == taker, spread(values), 0.0))
+    block = block_rows(order_ref[:group, :], me_ref)
+    ours = (block % n_ffn) == (me_ref[0] % n_ffn)
+    tok_place = jnp.where(ours, block // n_ffn, -1)
+    first = 4 * count + dpos.shape[1] // group
+    row = lax.broadcasted_iota(jnp.int32, (group, 1), 0) % unit
+    for n in range(16 // unit):
+        rows = slice(n * unit, (n + 1) * unit)
+        spread = lambda value: jnp.concatenate([value[rows]] * (group // unit), axis=0)
+        taker = jnp.where(row + n * unit < VECTORS, block, tok_place)
+        put(first + n, jnp.where(spread(taker_ref[...]) == taker, spread(values), 0.0))
 
 
 def weight_grads(
-    half, unit, me, order, rel_order, takers, x, rel, x_pick, c_pick, dpos, dq, dk, dv, dattn,
-    w_query, w_key, early, bins, *got
+    n_all, n_ffn, unit, me, order, rel_order, takers, x, rel, x_pick, c_pick, dpos, dq, dk, dv, dattn,
+    w_query, w_key, early, bins,
 ):
     width, seq = x.shape
     group = 2 * LANES
@@ -767,27 +755,24 @@
     col = lambda value: pl.BlockSpec((value.shape[0], group), lambda n: (0, n))
     row = lambda value: pl.BlockSpec((group, value.shape[1]), lambda n: (n, 0))
     plane = lambda t: pl.BlockSpec((1, dpos.shape[1], group), lambda n: (t, 0, n))
-    block = lambda rows: pl.BlockSpec((planes, rows, group), lambda n: (0, 0, n))
-    shape = lambda rows: jax.ShapeDtypeStruct((planes, rows, width), bf16)
-    rows = [LANES] if half else [LANES // 2] * 2
+    block = pl.BlockSpec((planes, LANES, group), lambda n: (0, 0, n))
     return pl.pallas_call(
-        functools.partial(grads_kernel, half, planes, unit),
+        functools.partial(grads_kernel, n_all, n_ffn, unit),
         grid=(width // group,),
         in_specs=[
             pl.BlockSpec(memory_space=pltpu.SMEM), whole(order), whole(rel_order), col(takers),
             whole(x), whole(rel), whole(x_pick), whole(c_pick), whole(dpos),
             col(dq), col(dk), col(dv), col(dattn), plane(0), plane(1), row(w_query), row(w_key),
             col(early), col(bins), pl.BlockSpec((8, group), lambda n: (0, n + width // group)),
-        ]
-        + [block(LANES) for _ in got],
-        out_specs=[block(count) for count in rows],
-        out_shape=[shape(count) for count in rows],
-        scratch_shapes=[pltpu.VMEM((2, dpos.shape[1] // 2, width), bf16)],
+        ],
+        out_specs=[block] * 2,
+        out_shape=[jax.ShapeDtypeStruct((planes, LANES, width), bf16)] * 2,
+        scratch_shapes=[pltpu.VMEM(dpos.shape, bf16)],
         compiler_params=PARAMS,
         name="weight_grads",
     )(
         me, order, rel_order, takers, x, rel, x_pick, c_pick, dpos, dq, dk, dv, dattn, dpos, dpos,
-        w_query, w_key, early, bins, bins, *got
+        w_query, w_key, early, bins, bins,
     )
 
 
@@ -874,7 +859,7 @@
     takers += [(spots + n * width) // (hidden_cols // n_tok) for n in range(hidden_cols // width)]
     takers = np.stack(takers).astype(np.int32)
     takers = jnp.asarray(np.pad(takers, ((0, 16 - takers.shape[0]), (0, 0)), constant_values=-2))
-    me = jnp.stack([over_all.me, over_all.upper, jnp.int32(n_all), jnp.int32(n_ffn)])
+    me = jnp.stack([over_all.me, over_all.upper])
     table_of = jnp.asarray(np.repeat(distance_rows(seq, table_rows)[:, None], LANES, 1))
 
     core = lax.axis_index("tok") % 2
@@ -897,7 +882,7 @@
     h1_theirs = swap(h1_mine, "ffn", 1)
     bias_theirs = swap(bias_row, "ffn", 1)
     x_turned, x_pick_turned, c_pick_turned, rel_turned = turn_blocks(
-        me, order, tokens, x_pick, ctx_pick, rel_table
+        n_all, me, order, tokens, x_pick, ctx_pick, rel_table
     )
     h1_both = jnp.concatenate([h1_mine, after(h1_theirs, x_turned)], axis=0)
     count = h1_mine.shape[0]
@@ -963,36 +948,35 @@
     )
     far_in, ffn_got = after((far_in, ffn_got), dk)
     ffn_kept, ffn_got = ffn_next(2, ffn_kept, ffn_got)
-
-    def grads(half, dk, *more):
-        return weight_grads(
-            half, unit, me, order, rel_order, takers,
-            x_turned, rel_turned, x_pick_turned, c_pick_turned, dpos, dq, dk, dv, dattn,
-            w_query, w_key, early, gb_in, *more,
-        )
-
-    (all_send,) = grads(1, after(dk, far_in, ffn_kept))
     near_in = swap(far_in, "tok", 1)
     far_down = swap(after(down_half, far_in), "ffn", 1)
-    all_got = over_all.send(all_send, 0)
-    grad_tokens = token_grads(pick, dz1, dq, after(dk, all_send), dv, w_query, w_key, w_value)
-    all_kept, all_sent = grads(0, after(dk, grad_tokens), all_got)
-    ffn_step = 3
+    all_kept, all_sent = weight_grads(
+        n_all, n_ffn, unit, me, order, rel_order, takers,
+        x_turned, rel_turned, x_pick_turned, c_pick_turned, dpos, dq, after(dk, far_in, ffn_kept), dv,
+        dattn, w_query, w_key, early, gb_in,
+    )
+    all_got = over_all.send(all_sent, 0)
+    ffn_kept, ffn_got = ffn_next(3, ffn_kept, after(ffn_got, all_sent))
+    dk_later, dq_later = after((dk, dq), all_sent, ffn_kept)
+    grad_tokens = token_grads(pick, dz1, dq_later, dk_later, dv, w_query, w_key, w_value)
+    all_kept, all_sent = next_halves(all_kept, after(all_got, grad_tokens), 1)
+    ffn_step = 4
 
     def attend(first, count, q):
         return attend_full(rel_ids, q, k, v, pos_key, key_scores, first, count)
 
     ctx = []
+    cuts = [(0, FIRST_PAIRS), (FIRST_PAIRS, pairs - FIRST_PAIRS)]
     for step in range(1, over_all.steps):
         all_got = over_all.send(all_sent, step)
-        if step == 1:
-            ctx.append(attend(0, FIRST_PAIRS, after(q, all_sent)))
-            fill = ctx[-1]
-        elif step == 2:
-            ctx.append(attend(FIRST_PAIRS, pairs - FIRST_PAIRS, after(q, all_sent)))
-            fill = ctx[-1]
-        elif step == 3:
-            near_down = swap(far_down, "tok", 1)
+        if step <= 2:
+            ctx.append(attend(*cuts[step - 1], after(q, all_sent)))
+            all_got = after(all_got, ctx[-1])
+            if step == 1:
+                far_down = after(far_down, ctx[-1])
+                near_down = swap(far_down, "tok", 1)
+                all_got = after(all_got, far_down)
+        elif step == 4:
             biases = [
                 lax.dynamic_slice_in_dim(bias_theirs, at * half_cols, half_cols, 1)
                 for at in (core, 1 - core)
@@ -1004,19 +988,17 @@
                 after(tokens, all_sent), ctx, w_out, b_out, ln1_gain, ln1_bias, shards,
                 b_down, ln2_gain, ln2_bias,
             )
-            fill = output
-        if step <= 3:
-            all_got = after(all_got, fill)
-        if step <= 2 and ffn_step <= over_tok.steps:
-            ffn_kept, ffn_got = ffn_next(ffn_step, ffn_kept, after(ffn_got, fill))
-            all_got = after(all_got, ffn_kept)
+            all_got = after(all_got, output)
+        if ffn_step <= over_tok.steps:
+            ffn_got = after(ffn_got, all_sent)
+            if step <= 2:
+                ffn_got = after(ffn_got, ctx[-1])
+            ffn_kept, ffn_got = ffn_next(ffn_step, ffn_kept, ffn_got)
             ffn_step += 1
         if step < over_all.steps - 1:
             all_kept, all_sent = next_halves(all_kept, all_got, 1)
         else:
             all_sums = add(all_kept, all_got)
-    for step in range(ffn_step, over_tok.steps + 1):
-        ffn_kept, ffn_got = ffn_next(step, ffn_kept, ffn_got)
 
     planes = 4 * (width // group) + table_rows // group
     vectors = wide(all_sums[planes:].reshape(16, width))

time: 238 us -> 236 us (level)
  Pallas kernels: 130 us -> 118 us
  waiting for transfers between devices: 33.2 us -> 41 us
  other arithmetic: 15.4 us -> 19 us
    pallas_call x3 -> x2, Pallas kernels: 28.4 us -> 16.7 us  [the longest x1 11.6 us: weight_grads(): pl.pallas_call(functools.partial(grads_kernel, n_all, n_ffn, unit), grid=...]
    ppermute x9, waiting for transfers between devices: 10.3 us -> 20.8 us  [swap(): return lax.ppermute(values, axis, [(n, n ^ bit) for n in range(size)])]
    convert_element_type x9 -> x10, other arithmetic: 10.4 us -> 14.1 us  [local(): low = lambda value: value.astype(bf16)]
    ppermute x13, waiting for transfers between devices: 23 us -> 20.2 us  [send(): return lax.ppermute(values, self.axes, pairs)]
  transfers between devices with their start and end apart: 22 -> 22, of which waited for: 8 -> 12; matrix products, arithmetic and copies ran while one was open for 9% -> 7% of each run, Pallas kernels for 32% -> 32%
where the time goes in v1:
time: 236 us; the launch traced here: 233 us
  Pallas kernels  118 us (50%)
  waiting for transfers between devices  41 us (17%)
  matrix products  23.5 us (10%)
  other arithmetic  19 us (8%)
  starting transfers between devices  18.2 us (8%)
  local copies, waits for them, and re-layouts  12.1 us (5%)
    pallas_call x1, Pallas kernels, attend_picked(): pl.pallas_call(picked_kernel, grid=(pairs,), in_specs=[pl.BlockSpec(memor...  30.3 us
    pallas_call x2, Pallas kernels, attend_full(): pl.pallas_call(full_kernel, grid=(pairs // per,), in_specs=[pl.BlockSpec(...  27 us
    pallas_call x1, Pallas kernels, attend_back(): pl.pallas_call(back_kernel, grid=(pairs,), in_specs=[whole(table_of), who...  24.5 us
    ppermute x9, waiting for transfers between devices, swap(): return lax.ppermute(values, axis, [(n, n ^ bit) for n in range(size)])  20.8 us
    ppermute x13, waiting for transfers between devices, send(): return lax.ppermute(values, self.axes, pairs)  20.2 us
    dot_general x12, matrix products, dot_nn(): lax.dot_general(first_op, second_op, (((1,), (0,)), ((), ())), preferred_...  16.3 us
    convert_element_type x10, other arithmetic, local(): low = lambda value: value.astype(bf16)  14.1 us
    ppermute x13, starting transfers between devices, send(): return lax.ppermute(values, self.axes, pairs)  12.6 us
  transfers between devices with their start and end apart: 22, of which 12 were waited for; matrix products, arithmetic and copies ran while one was open for 7% of the time, Pallas kernels for 32%

profile of v1, /device:TPU:0, one launch (start us, length us, event | category | flops | bytes accessed | tf_op | source)
XLA Modules:
  0.0 232.7 jit_solution(6841164588414189123)
XLA Ops:
  0.7 1.5 convolution_convert_fusion.5.x_ref.xpick_ref
  2.2 3.3 %add_convert_fusion.8.k_ref = bf16[512,768]{1,0:T(8,128)(2,1)} fusion(bf16[512,768]{1,0:T(8,128)(2,1)} %x_ref.2, bf16[768,768]{1,0:T(8,128)(2,1)} %wk_ref.3, f32[768]{0:T(1024)} %param.37), kind=kOutput, calls=%fused_computation.16 | convolution fusion | flops 604766208 | bytes 2755584 | tf_op jit(solution)/shard_map/dot_general | solution.py:27
  5.5 1.7 add_convert_fusion.6.pk_ref
  7.2 1.7 add_convert_fusion.5.pq_ref
  8.9 1.0 fusion.5.qc_ref
  9.9 1.7 add_convert_fusion.7.v_ref
  11.6 30.3 %attend_picked.1 = (bf16[80,768]{1,0:T(8,128)(2,1)}, bf16[12,80,512]{2,1,0:T(8,128)(2,1)}, f32[12,512,512]{2,1,0:T(8,128)}, s32[512,128]{1,0:T(8,128)}, s32[80,1...) custom-call(s32[80]{0:T(128)} %bitcast.98, s32[512,512]{1,0:T(8,128)} %bitcast.91, ...), custom_call_target="tpu_custom_call" | custom-call | tf_op jit(solution)/shard_map/attend_picked/pallas_call | solution.py:277
  41.8 3.0 %collective-permute-start = (bf16[80,768]{1,0:T(8,128)(2,1)}, bf16[80,768]{1,0:T(8,128)(2,1)}, u32[]{:S(2)}, u32[]{:S(2)}) collective-permute-start(bf16[80,768]{1,0:T(8,128)(2,1)} %get-tuple-element.87), channel_id=1, source_target_pairs={{0,1},{1,0},{2,3},{3,2},{4,5},{5,4},{6,7},{7,6},{8,9},{9,8},{10,11... | collective-permute-start | bytes 368648 | tf_op jit(solution)/shard_map/ppermute | solution.py:781
  44.8 0.7 fusion.10.pick_ref
  45.6 0.7 multiply_add_fusion
  46.3 1.4 fusion.2
  47.7 1.1 constant_dynamic-slice_fusion.5
  49.4 5.1 %turn_blocks.1 = (bf16[768,512]{1,0:T(8,128)(2,1)}, bf16[768,80]{1,0:T(8,128)(2,1)}, bf16[768,80]{1,0:T(8,128)(2,1)}, bf16[768,512]{1,0:T(8,128)(2,1)}) custom-call(s32[2]{0:T(128)} %pad_add_fusion.me_ref, s32[768,128]{1,0:T(8,128)} %constant.86.clone.order_ref, bf16[512,768]{1,0:T(8,128)(2,1)} %x_ref.2, bf16[80,768]{1,0:T(8,128)(2,1)} %copy-done.9, ...), custom_call_target="tpu_custom_call" | custom-call | tf_op jit(solution)/shard_map/turn_blocks/pallas_call | solution.py:558
  54.5 0.9 constant_dynamic-update-slice_fusion
  55.5 1.6 multiply_convert_fusion
  57.8 0.7 fusion.42
  58.5 1.7 add_convert_fusion.4.q_ref
  60.6 4.5 %collective-permute-done.1.got_ref = bf16[80,768]{1,0:T(8,128)(2,1)S(1)} collective-permute-done((bf16[80,768]{1,0:T(8,128)(2,1)S(1)}, bf16[80,768]{1,0:T(8,128)(2,1)S(1)}, u32[]{:S(2)}, u32[]{:S(2)}) %collective-permute-start.1) | collective-permute-done | bytes 122912 | tf_op jit(solution)/shard_map/ppermute | solution.py:781
  65.0 0.6 copy-done.19
  65.7 2.4 %norm_picked.1 = (f32[80,768]{1,0:T(8,128)}, bf16[80,768]{1,0:T(8,128)(2,1)}, f32[8,768]{1,0:T(8,128)}) custom-call(f32[80,768]{1,0:T(8,128)} %get-tuple-element.86.normed_ref, f32[768]{0:T(1024)} %gain1_ref.3, f32[768]{0:T(1024)} %bias1_ref.3, bf16[80,768]{1,0:T(8,128)(2,1)} %get-tuple-element.154.mine_ref, bf16[80,768]{1,0:T(8,128)(2,1)} %copy-done.19, ...), custom_call_target="tpu_custom_call" | custom-call | tf_op jit(solution)/shard_map/norm_picked/pallas_call | solution.py:590
  68.3 2.5 %constant_dynamic-slice_fusion.4 = bf16[768,768]{1,0:T(8,128)(2,1)} fusion(bf16[1536,768]{1,0:T(8,128)(2,1)} %down_ref.1, s32[]{:T(128)S(6)} %select_n.45), kind=kLoop, calls=%fused_computation.90 | loop fusion | bytes 2359300 | tf_op jit(solution)/shard_map/dynamic_slice | solution.py:869
  70.8 0.9 constant_dynamic-update-slice_fusion.3
  71.8 1.4 collective-permute-done.2
  73.2 2.2 fusion
  75.4 0.9 convolution_convert_fusion.3
  76.3 0.7 fusion.41
  77.0 0.6 fusion.3
  78.9 4.1 %collective-permute-done.3.got_ref = bf16[80,768]{1,0:T(8,128)(2,1)S(1)} collective-permute-done((bf16[80,768]{1,0:T(8,128)(2,1)S(1)}, bf16[80,768]{1,0:T(8,128)(2,1)S(1)}, u32[]{:S(2)}, u32[]{:S(2)}) %collective-permute-start.3) | collective-permute-done | bytes 122912 | tf_op jit(solution)/shard_map/ppermute | solution.py:781
  83.8 2.1 collective-permute-done.5
  85.9 1.2 add_convert_fusion.11
  87.1 1.5 collective-permute-start.8
  88.6 1.3 add_convert_fusion.12
  90.4 0.8 fusion.37.bin_ref.bin2_ref
  91.9 24.5 %attend_back.1 = (bf16[80,768]{1,0:T(8,128)(2,1)}, bf16[512,768]{1,0:T(8,128)(2,1)}, bf16[512,768]{1,0:T(8,128)(2,1)}, bf16[2,512,768]{2,1,0:T(8,128)(2,1)}, f32...) custom-call(s32[1024,128]{1,0:T(8,128)} %constant.89.clone.row_ref, ...), custom_call_target="tpu_custom_call" | custom-call | tf_op jit(solution)/shard_map/attend_back/pallas_call | solution.py:494
  116.5 1.6 add_convert_fusion.15
  118.1 1.9 add_convert_fusion.16
  120.0 11.6 %weight_grads.1 = (bf16[16,128,768]{2,1,0:T(8,128)(2,1)}, bf16[16,128,768]{2,1,0:T(8,128)(2,1)}) custom-call(s32[2]{0:T(128)} %pad_add_fusion.me_ref, s32[768,128]{1,0:T(8,128)} %constant.86.clone.order_ref, s32[512,128]{1,0:T(8,128)} %constant.87.clone.relorder_ref, s32[16,768]{1,0:T(8,128)} %constant.88.clone.taker_ref, ...), custom_call_target="tpu_custom_call" | custom-call | tf_op jit(solution)/shard_map/weight_grads/pallas_call | solution.py:759
  131.6 1.6 collective-permute-start.11
  133.7 4.7 %collective-permute-done.11 = bf16[96,1536]{1,0:T(8,128)(2,1)S(1)} collective-permute-done((bf16[96,1536]{1,0:T(8,128)(2,1)S(1)}, bf16[96,1536]{1,0:T(8,128)(2,1)S(1)}, u32[]{:S(2)}, u32[]{:S(2)}) %collective-permute-start.11) | collective-permute-done | bytes 294944 | tf_op jit(solution)/shard_map/ppermute | solution.py:805
  138.4 3.2 %collective-permute-done.10 = bf16[96,1536]{1,0:T(8,128)(2,1)S(1)} collective-permute-done((bf16[96,1536]{1,0:T(8,128)(2,1)}, bf16[96,1536]{1,0:T(8,128)(2,1)S(1)}, u32[]{:S(2)}, u32[]{:S(2)}) %collective-permute-start.10) | collective-permute-done | bytes 294944 | tf_op jit(solution)/shard_map/ppermute | solution.py:805
  141.6 0.7 add_convert_fusion.24
  142.3 0.7 add_convert_fusion.25
  143.1 5.9 %token_grads.1 = f32[512,768]{1,0:T(8,128)} custom-call(bf16[80,512]{1,0:T(8,128)(2,1)} %fusion.10.pick_ref, f32[80,768]{1,0:T(8,128)} %get-tuple-element.117.dz1_ref, bf16[80,768]{1,0:T(8,128)(2,1)} %get-tuple-element.120.dq_ref, bf16[512,768]{1,0:T(8,128)(2,1)} %get-tuple-element.121.dk_ref, bf16[512,768]{1,0:T(8,128)(2,1)} %get-tuple-element.112.dv_ref, ...), custom_call_target="tpu_custom_call" | custom-call | tf_op jit(solution)/shard_map/token_grads/pallas_call | solution.py:683
  149.0 1.6 copy-done.8
  150.6 4.1 %add_convert_fusion = (bf16[16,64,768]{2,1,0:T(8,128)(2,1)S(1)}, bf16[16,64,768]{2,1,0:T(8,128)(2,1)S(1)}) fusion(bf16[16,128,768]{2,1,0:T(8,128)(2,1)} %copy-done.8, bf16[16,128,768]{2,1,0:T(8,128)(2,1)} %get-tuple-element.115), kind=kLoop, calls=%fused_computation | loop fusion | flops 6291456 | bytes 9437184 | tf_op jit(solution)/shard_map/convert_element_type | solution.py:845
  154.7 1.6 collective-permute-start.12
  156.8 16.9 %attend_full.2.ctx_ref = bf16[512,512]{1,0:T(8,128)(2,1)} custom-call(s32[512,512]{1,0:T(8,128)} %bitcast.92, bf16[512,768]{1,0:T(8,128)(2,1)} %add_convert_fusion.4.q_ref, bf16[512,768]{1,0:T(8,128)(2,1)} %add_convert_fusion.8.k_ref, bf16[512,768]{1,0:T(8,128)(2,1)} %add_convert_fusion.7.v_ref, bf16[512,768]{1,0:T(8,128)(2,1)} %add_convert_fusion.6.pk_ref, ...), custom_call_target="tpu_custom_call" | custom-call | tf_op jit(solution)/shard_map/attend_full/pallas_call | solution.py:368
  173.7 10.1 %collective-permute-done.13.down2_ref = bf16[768,768]{1,0:T(8,128)(2,1)} collective-permute-done((bf16[768,768]{1,0:T(8,128)(2,1)}, bf16[768,768]{1,0:T(8,128)(2,1)}, u32[]{:S(2)}, u32[]{:S(2)}) %collective-permute-start.13) | collective-permute-done | bytes 1179680 | tf_op jit(solution)/shard_map/ppermute | solution.py:781
  183.8 2.9 %add_convert_fusion.2 = (bf16[16,32,768]{2,1,0:T(8,128)(2,1)}, bf16[16,32,768]{2,1,0:T(8,128)(2,1)S(1)}) fusion(bf16[16,64,768]{2,1,0:T(8,128)(2,1)S(1)} %get-tuple-element.138, bf16[16,64,768]{2,1,0:T(8,128)(2,1)} %collective-permute-done.12), kind=kLoop, calls=%fused_computation.10 | loop fusion | flops 3145728 | bytes 4718592 | tf_op jit(solution)/shard_map/convert_element_type | solution.py:845
  187.8 10.2 %attend_full.3.ctx2_ref = bf16[512,256]{1,0:T(8,128)(2,1)} custom-call(s32[512,512]{1,0:T(8,128)} %bitcast.93, bf16[512,768]{1,0:T(8,128)(2,1)} %add_convert_fusion.4.q_ref, bf16[512,768]{1,0:T(8,128)(2,1)} %add_convert_fusion.8.k_ref, bf16[512,768]{1,0:T(8,128)(2,1)} %add_convert_fusion.7.v_ref, bf16[512,768]{1,0:T(8,128)(2,1)} %add_convert_fusion.6.pk_ref, ...), custom_call_target="tpu_custom_call" | custom-call | tf_op jit(solution)/shard_map/attend_full/pallas_call | solution.py:368
  198.0 0.9 collective-permute-done.14
  198.9 0.9 copy-done.15
  199.8 1.3 add_convert_fusion.14
  202.2 2.6 %collective-permute-start.21 = (bf16[48,1536]{1,0:T(8,128)(2,1)S(1)}, bf16[48,1536]{1,0:T(8,128)(2,1)S(1)}, u32[]{:S(2)}, u32[]{:S(2)}) collective-permute-start(bf16[48,1536]{1,0:T(8,128)(2,1)S(1)} %copy-done.16), channel_id=1, source_target_pairs={{0,16},{2,18},{4,20},{6,22},{8,24},{10,26},{12,28},{14,30},{16,0},... | collective-permute-start | bytes 442376 | tf_op jit(solution)/shard_map/ppermute | solution.py:805
  204.8 0.6 collective-permute-done.16
  205.5 2.6 %collective-permute-start.20 = (bf16[48,1536]{1,0:T(8,128)(2,1)}, bf16[48,1536]{1,0:T(8,128)(2,1)S(1)}, u32[]{:S(2)}, u32[]{:S(2)}) collective-permute-start(bf16[48,1536]{1,0:T(8,128)(2,1)} %get-tuple-element.149), channel_id=1, source_target_pairs={{0,16},{2,18},{4,20},{6,22},{8,24},{10,26},{12,28},{14,30},{16,0},... | collective-permute-start | bytes 442376 | tf_op jit(solution)/shard_map/ppermute | solution.py:805
  208.7 1.4 collective-permute-done.21
  210.1 7.0 %collective-permute-done.20 = bf16[48,1536]{1,0:T(8,128)(2,1)S(1)} collective-permute-done((bf16[48,1536]{1,0:T(8,128)(2,1)}, bf16[48,1536]{1,0:T(8,128)(2,1)S(1)}, u32[]{:S(2)}, u32[]{:S(2)}) %collective-permute-start.20) | collective-permute-done | bytes 147488 | tf_op jit(solution)/shard_map/ppermute | solution.py:805
  217.2 0.9 convert_bitcast_fusion
  218.1 10.8 %ffn_full.1 = bf16[512,768]{1,0:T(8,128)(2,1)} custom-call(bf16[512,768]{1,0:T(8,128)(2,1)} %x_ref.2, bf16[512,512]{1,0:T(8,128)(2,1)} %attend_full.2.ctx_ref, bf16[512,256]{1,0:T(8,128)(2,1)} %attend_full.3.ctx2_ref, bf16[768,768]{1,0:T(8,128)(2,1)} %wo_ref.5, f32[768]{0:T(1024)} %bo_ref.3, f32[768]{0:T(1024)} %gain1_ref.3, f32[768]{0:T(1024)} %bias1_ref.3, ...), custom_call_target="tpu_custom_call" | custom-call | tf_op jit(solution)/shard_map/ffn_full/pallas_call | solution.py:649
  229.0 0.9 collective-permute-done.19
  230.0 0.7 fusion.31
  230.7 0.6 fusion.35
  231.9 0.6 dynamic-slice_bitcast_fusion
  (93 shorter events, 10.1 us)
Async XLA Ops:
  2.1 6.8 %copy-start.9 = (bf16[80,768]{1,0:T(8,128)(2,1)}, bf16[80,768]{1,0:T(8,128)(2,1)S(1)}, u32[]{:S(2)}) copy-start(bf16[80,768]{1,0:T(8,128)(2,1)S(1)} %convolution_convert_fusion.5.x_ref.xpick_ref) | copy-start | bytes 368644
  2.1 3.4 %copy-start.6 = (bf16[768,768]{1,0:T(8,128)(2,1)S(1)}, bf16[768,768]{1,0:T(8,128)(2,1)}, u32[]{:S(2)}) copy-start(bf16[768,768]{1,0:T(8,128)(2,1)} %wk_ref.3) | copy-start | bytes 3538948
  2.1 3.4 %copy-start.14 = (bf16[512,768]{1,0:T(8,128)(2,1)S(1)}, bf16[512,768]{1,0:T(8,128)(2,1)}, u32[]{:S(2)}) copy-start(bf16[512,768]{1,0:T(8,128)(2,1)} %rel_ref.1) | copy-start | bytes 2359300
  2.1 3.3 %copy-start.25 = (f32[768]{0:T(1024)S(1)}, f32[768]{0:T(1024)}, u32[]{:S(2)}) copy-start(f32[768]{0:T(1024)} %param.37) | copy-start | bytes 9220
  5.5 1.7 copy-start.3
  5.5 1.7 copy-start.23
  7.2 2.7 %copy-start.4 = (bf16[512,768]{1,0:T(8,128)(2,1)S(1)}, bf16[512,768]{1,0:T(8,128)(2,1)}, u32[]{:S(2)}) copy-start(bf16[512,768]{1,0:T(8,128)(2,1)} %x_ref.2) | copy-start | bytes 2359300
  7.2 2.7 %copy-start.13 = (bf16[768,768]{1,0:T(8,128)(2,1)S(1)}, bf16[768,768]{1,0:T(8,128)(2,1)}, u32[]{:S(2)}) copy-start(bf16[768,768]{1,0:T(8,128)(2,1)} %wv_ref.1) | copy-start | bytes 3538948
  7.2 2.7 %copy-start.26 = (f32[768]{0:T(1024)S(1)}, f32[768]{0:T(1024)}, u32[]{:S(2)}) copy-start(f32[768]{0:T(1024)} %param.38) | copy-start | bytes 9220
  11.5 33.3 %copy-start.22 = (s32[1,80]{1,0:T(1,128)S(1)}, s32[1,80]{1,0:T(1,128)}, u32[]{:S(2)}) copy-start(s32[1,80]{1,0:T(1,128)} %param.30) | copy-start | bytes 964
  11.6 34.0 %copy-start.24 = (s32[768]{0:T(1024)S(1)}, s32[768]{0:T(1024)}, u32[]{:S(2)}) copy-start(s32[768]{0:T(1024)} %constant.90.clone) | copy-start | bytes 9220
  11.6 36.1 %copy-start = (bf16[768,1536]{1,0:T(8,128)(2,1)S(1)}, bf16[768,1536]{1,0:T(8,128)(2,1)}, u32[]{:S(2)}) copy-start(bf16[768,1536]{1,0:T(8,128)(2,1)} %win_ref.1) | copy-start | bytes 7077892
  41.8 12.7 %collective-permute-start = (bf16[80,768]{1,0:T(8,128)(2,1)}, bf16[80,768]{1,0:T(8,128)(2,1)}, u32[]{:S(2)}, u32[]{:S(2)}) collective-permute-start(bf16[80,768]{1,0:T(8,128)(2,1)} %get-tuple-element.87), channel_id=1, source_target_pairs={{0,1},{1,0},{2,3},{3,2},{4,5},{5,4},{6,7},{7,6},{8,9},{9,8},{10,11... | collective-permute-start | bytes 368648 | tf_op jit(solution)/shard_map/ppermute | solution.py:781
  48.8 5.7 %copy-start.17 = (bf16[80,768]{1,0:T(8,128)(2,1)S(1)}, bf16[80,768]{1,0:T(8,128)(2,1)}, u32[]{:S(2)}) copy-start(bf16[80,768]{1,0:T(8,128)(2,1)} %get-tuple-element.87) | copy-start | bytes 368644
  48.8 6.7 %copy-start.20 = (f32[1536]{0:T(1024)S(1)}, f32[1536]{0:T(1024)}, u32[]{:S(2)}) copy-start(f32[1536]{0:T(1024)} %param.44) | copy-start | bytes 18436
  55.5 1.8 copy-start.1
  57.3 1.2 copy-start.5
  58.5 1.7 copy-start.7
  60.2 4.9 %collective-permute-start.1 = (bf16[80,768]{1,0:T(8,128)(2,1)S(1)}, bf16[80,768]{1,0:T(8,128)(2,1)S(1)}, u32[]{:S(2)}, u32[]{:S(2)}) collective-permute-start(bf16[80,768]{1,0:T(8,128)(2,1)S(1)} %get-tuple-element.153), channel_id=1, source_target_pairs={{0,1},{1,0},{2,3},{3,2},{4,5},{5,4},{6,7},{7,6},{8,9},{9,8},{10,11... | collective-permute-start | bytes 368648 | tf_op jit(solution)/shard_map/ppermute | solution.py:781
  65.0 0.7 copy-start.19
  68.1 5.1 %copy-start.2 = (bf16[1536,768]{1,0:T(8,128)(2,1)S(1)}, bf16[1536,768]{1,0:T(8,128)(2,1)}, u32[]{:S(2)}) copy-start(bf16[1536,768]{1,0:T(8,128)(2,1)} %down_ref.1) | copy-start | bytes 7077892
  68.1 5.1 %collective-permute-start.2 = (bf16[80,768]{1,0:T(8,128)(2,1)}, bf16[80,768]{1,0:T(8,128)(2,1)S(1)}, u32[]{:S(2)}, u32[]{:S(2)}) collective-permute-start(bf16[80,768]{1,0:T(8,128)(2,1)} %get-tuple-element.93), channel_id=1, source_target_pairs={{0,1},{1,0},{2,3},{3,2},{4,5},{5,4},{6,7},{7,6},{8,9},{9,8},{10,11... | collective-permute-start | bytes 368648 | tf_op jit(solution)/shard_map/ppermute | solution.py:781
  77.6 6.0 %copy-start.12 = (bf16[768,768]{1,0:T(8,128)(2,1)S(1)}, bf16[768,768]{1,0:T(8,128)(2,1)}, u32[]{:S(2)}) copy-start(bf16[768,768]{1,0:T(8,128)(2,1)} %constant_dynamic-slice_fusion.5) | copy-start | bytes 3538948
  78.1 4.9 %collective-permute-start.3 = (bf16[80,768]{1,0:T(8,128)(2,1)S(1)}, bf16[80,768]{1,0:T(8,128)(2,1)S(1)}, u32[]{:S(2)}, u32[]{:S(2)}) collective-permute-start(bf16[80,768]{1,0:T(8,128)(2,1)S(1)} %get-tuple-element.151), channel_id=1, source_target_pairs={{0,1},{1,0},{2,3},{3,2},{4,5},{5,4},{6,7},{7,6},{8,9},{9,8},{10,11... | collective-permute-start | bytes 368648 | tf_op jit(solution)/shard_map/ppermute | solution.py:781
  83.0 6.8 %copy-start.18 = (bf16[80,768]{1,0:T(8,128)(2,1)}, bf16[80,768]{1,0:T(8,128)(2,1)S(1)}, u32[]{:S(2)}) copy-start(bf16[80,768]{1,0:T(8,128)(2,1)S(1)} %collective-permute-done.3.got_ref) | copy-start | bytes 368644
  83.0 2.8 %collective-permute-start.5 = (bf16[384,1536]{1,0:T(8,128)(2,1)S(1)}, bf16[384,1536]{1,0:T(8,128)(2,1)S(1)}, u32[]{:S(2)}, u32[]{:S(2)}) collective-permute-start(bf16[384,1536]{1,0:T(8,128)(2,1)S(1)} %convolution_convert_fusion), channel_id=1, source_target_pairs={{0,2},{2,0},{4,6},{6,4},{8,10},{10,8},{12,14},{14,12},{16,18},{18,... | collective-permute-start | bytes 3538952 | tf_op jit(solution)/shard_map/ppermute | solution.py:805
  83.0 5.6 %collective-permute-start.4 = (bf16[384,1536]{1,0:T(8,128)(2,1)S(1)}, bf16[384,1536]{1,0:T(8,128)(2,1)S(1)}, u32[]{:S(2)}, u32[]{:S(2)}) collective-permute-start(bf16[384,1536]{1,0:T(8,128)(2,1)S(1)} %convolution_convert_fusion.1), channel_id=1, source_target_pairs={{0,2},{2,0},{4,6},{6,4},{8,10},{10,8},{12,14},{14,12},{16,18},{18,... | collective-permute-start | bytes 3538952 | tf_op jit(solution)/shard_map/ppermute | solution.py:805
  83.6 32.9 %collective-permute-start.6 = (bf16[768,768]{1,0:T(8,128)(2,1)S(1)}, bf16[768,768]{1,0:T(8,128)(2,1)S(1)}, u32[]{:S(2)}, u32[]{:S(2)}) collective-permute-start(bf16[768,768]{1,0:T(8,128)(2,1)S(1)} %copy-done.12), channel_id=1, source_target_pairs={{0,1},{1,0},{2,3},{3,2},{4,5},{5,4},{6,7},{7,6},{8,9},{9,8},{10,11... | collective-permute-start | bytes 3538952 | tf_op jit(solution)/shard_map/ppermute | solution.py:781
  87.1 29.3 %collective-permute-start.8 = (bf16[192,1536]{1,0:T(8,128)(2,1)}, bf16[192,1536]{1,0:T(8,128)(2,1)}, u32[]{:S(2)}, u32[]{:S(2)}) collective-permute-start(bf16[192,1536]{1,0:T(8,128)(2,1)} %add_convert_fusion.11), channel_id=1, source_target_pairs={{0,4},{2,10},{4,0},{6,14},{8,12},{10,2},{12,8},{14,6},{16,20},{18,... | collective-permute-start | bytes 1769480 | tf_op jit(solution)/shard_map/ppermute | solution.py:805
  89.9 26.6 %collective-permute-start.7 = (bf16[192,1536]{1,0:T(8,128)(2,1)}, bf16[192,1536]{1,0:T(8,128)(2,1)}, u32[]{:S(2)}, u32[]{:S(2)}) collective-permute-start(bf16[192,1536]{1,0:T(8,128)(2,1)} %add_convert_fusion.12), channel_id=1, source_target_pairs={{0,4},{2,10},{4,0},{6,14},{8,12},{10,2},{12,8},{14,6},{16,20},{18,... | collective-permute-start | bytes 1769480 | tf_op jit(solution)/shard_map/ppermute | solution.py:805
  116.4 3.5 %copy-start.10 = (bf16[768,768]{1,0:T(8,128)(2,1)}, bf16[768,768]{1,0:T(8,128)(2,1)S(1)}, u32[]{:S(2)}) copy-start(bf16[768,768]{1,0:T(8,128)(2,1)S(1)} %collective-permute-done.6.win2_ref) | copy-start | bytes 3538948
  131.6 17.4 %collective-permute-start.9 = (bf16[16,128,768]{2,1,0:T(8,128)(2,1)}, bf16[16,128,768]{2,1,0:T(8,128)(2,1)S(1)}, u32[]{:S(2)}, u32[]{:S(2)}) collective-permute-start(bf16[16,128,768]{2,1,0:T(8,128)(2,1)} %get-tuple-element.116), channel_id=1, source_target_pairs={{0,2},{1,3},{2,0},{3,1},{4,6},{5,7},{6,4},{7,5},{8,10},{9,11},{10,... | collective-permute-start | bytes 9437192 | tf_op jit(solution)/shard_map/ppermute | solution.py:805
  131.6 6.8 %collective-permute-start.11 = (bf16[96,1536]{1,0:T(8,128)(2,1)S(1)}, bf16[96,1536]{1,0:T(8,128)(2,1)S(1)}, u32[]{:S(2)}, u32[]{:S(2)}) collective-permute-start(bf16[96,1536]{1,0:T(8,128)(2,1)S(1)} %get-tuple-element.143), channel_id=1, source_target_pairs={{0,8},{2,6},{4,12},{6,2},{8,0},{10,14},{12,4},{14,10},{16,24},{18,... | collective-permute-start | bytes 884744 | tf_op jit(solution)/shard_map/ppermute | solution.py:805
  133.3 8.3 %collective-permute-start.10 = (bf16[96,1536]{1,0:T(8,128)(2,1)}, bf16[96,1536]{1,0:T(8,128)(2,1)S(1)}, u32[]{:S(2)}, u32[]{:S(2)}) collective-permute-start(bf16[96,1536]{1,0:T(8,128)(2,1)} %get-tuple-element.145), channel_id=1, source_target_pairs={{0,8},{2,6},{4,12},{6,2},{8,0},{10,14},{12,4},{14,10},{16,24},{18,... | collective-permute-start | bytes 884744 | tf_op jit(solution)/shard_map/ppermute | solution.py:805
  149.0 1.6 copy-start.8
  154.7 29.1 %collective-permute-start.12 = (bf16[16,64,768]{2,1,0:T(8,128)(2,1)S(1)}, bf16[16,64,768]{2,1,0:T(8,128)(2,1)}, u32[]{:S(2)}, u32[]{:S(2)}) collective-permute-start(bf16[16,64,768]{2,1,0:T(8,128)(2,1)S(1)} %get-tuple-element.137), channel_id=1, source_target_pairs={{0,4},{1,5},{2,10},{3,11},{4,0},{5,1},{6,14},{7,15},{8,12},{9,13},... | collective-permute-start | bytes 4718600 | tf_op jit(solution)/shard_map/ppermute | solution.py:805
  156.2 27.6 %collective-permute-start.13 = (bf16[768,768]{1,0:T(8,128)(2,1)}, bf16[768,768]{1,0:T(8,128)(2,1)}, u32[]{:S(2)}, u32[]{:S(2)}) collective-permute-start(bf16[768,768]{1,0:T(8,128)(2,1)} %constant_dynamic-slice_fusion.4), channel_id=1, source_target_pairs={{0,1},{1,0},{2,3},{3,2},{4,5},{5,4},{6,7},{7,6},{8,9},{9,8},{10,11... | collective-permute-start | bytes 3538952 | tf_op jit(solution)/shard_map/ppermute | solution.py:781
  183.8 3.5 %copy-start.11 = (bf16[768,768]{1,0:T(8,128)(2,1)S(1)}, bf16[768,768]{1,0:T(8,128)(2,1)}, u32[]{:S(2)}) copy-start(bf16[768,768]{1,0:T(8,128)(2,1)} %copy-done.10) | copy-start | bytes 3538948
  186.7 12.2 %collective-permute-start.14 = (bf16[16,32,768]{2,1,0:T(8,128)(2,1)}, bf16[16,32,768]{2,1,0:T(8,128)(2,1)S(1)}, u32[]{:S(2)}, u32[]{:S(2)}) collective-permute-start(bf16[16,32,768]{2,1,0:T(8,128)(2,1)} %get-tuple-element.139), channel_id=1, source_target_pairs={{0,1},{1,0},{2,6},{3,7},{4,5},{5,4},{6,2},{7,3},{8,9},{9,8},{10,14... | collective-permute-start | bytes 2359304 | tf_op jit(solution)/shard_map/ppermute | solution.py:805
  187.3 30.8 %collective-permute-start.17 = (bf16[768,768]{1,0:T(8,128)(2,1)S(1)}, bf16[768,768]{1,0:T(8,128)(2,1)}, u32[]{:S(2)}, u32[]{:S(2)}) collective-permute-start(bf16[768,768]{1,0:T(8,128)(2,1)S(1)} %copy-done.11), channel_id=1, source_target_pairs={{0,2},{2,0},{4,6},{6,4},{8,10},{10,8},{12,14},{14,12},{16,18},{18,... | collective-permute-start | bytes 3538952 | tf_op jit(solution)/shard_map/ppermute | solution.py:781
  187.5 30.7 %collective-permute-start.18 = (bf16[768,768]{1,0:T(8,128)(2,1)}, bf16[768,768]{1,0:T(8,128)(2,1)}, u32[]{:S(2)}, u32[]{:S(2)}) collective-permute-start(bf16[768,768]{1,0:T(8,128)(2,1)} %collective-permute-done.13.down2_ref), channel_id=1, source_target_pairs={{0,2},{2,0},{4,6},{6,4},{8,10},{10,8},{12,14},{14,12},{16,18},{18,... | collective-permute-start | bytes 3538952 | tf_op jit(solution)/shard_map/ppermute | solution.py:781
  198.0 4.2 %copy-start.16 = (bf16[48,1536]{1,0:T(8,128)(2,1)S(1)}, bf16[48,1536]{1,0:T(8,128)(2,1)}, u32[]{:S(2)}) copy-start(bf16[48,1536]{1,0:T(8,128)(2,1)} %get-tuple-element.147) | copy-start | bytes 442372
  198.9 0.9 copy-start.15
  201.1 16.0 %collective-permute-start.15 = (bf16[16,16,768]{2,1,0:T(8,128)(2,1)S(1)}, bf16[16,16,768]{2,1,0:T(8,128)(2,1)S(1)}, u32[]{:S(2)}, u32[]{:S(2)}) collective-permute-start(bf16[16,16,768]{2,1,0:T(8,128)(2,1)S(1)} %get-tuple-element.142), channel_id=1, source_target_pairs={{0,8},{1,9},{2,3},{3,2},{4,12},{5,13},{6,7},{7,6},{8,0},{9,1},{10,... | collective-permute-start | bytes 1179656 | tf_op jit(solution)/shard_map/ppermute | solution.py:805
  201.6 16.5 %copy-start.21 = (f32[1,1536]{1,0:T(1,128)}, f32[1,1536]{1,0:T(1,128)S(1)}, u32[]{:S(2)}) copy-start(f32[1,1536]{1,0:T(1,128)S(1)} %broadcast_in_dim.5.bin_ref) | copy-start | bytes 18436
  201.6 3.8 %collective-permute-start.16 = (f32[1,1536]{1,0:T(1,128)S(1)}, f32[1,1536]{1,0:T(1,128)S(1)}, u32[]{:S(2)}, u32[]{:S(2)}) collective-permute-start(f32[1,1536]{1,0:T(1,128)S(1)} %broadcast_in_dim.5.bin_ref), channel_id=1, source_target_pairs={{0,1},{1,0},{2,3},{3,2},{4,5},{5,4},{6,7},{7,6},{8,9},{9,8},{10,11... | collective-permute-start | bytes 18440 | tf_op jit(solution)/shard_map/ppermute | solution.py:781
  202.2 7.9 %collective-permute-start.21 = (bf16[48,1536]{1,0:T(8,128)(2,1)S(1)}, bf16[48,1536]{1,0:T(8,128)(2,1)S(1)}, u32[]{:S(2)}, u32[]{:S(2)}) collective-permute-start(bf16[48,1536]{1,0:T(8,128)(2,1)S(1)} %copy-done.16), channel_id=1, source_target_pairs={{0,16},{2,18},{4,20},{6,22},{8,24},{10,26},{12,28},{14,30},{16,0},... | collective-permute-start | bytes 442376 | tf_op jit(solution)/shard_map/ppermute | solution.py:805
  205.5 11.6 %collective-permute-start.20 = (bf16[48,1536]{1,0:T(8,128)(2,1)}, bf16[48,1536]{1,0:T(8,128)(2,1)S(1)}, u32[]{:S(2)}, u32[]{:S(2)}) collective-permute-start(bf16[48,1536]{1,0:T(8,128)(2,1)} %get-tuple-element.149), channel_id=1, source_target_pairs={{0,16},{2,18},{4,20},{6,22},{8,24},{10,26},{12,28},{14,30},{16,0},... | collective-permute-start | bytes 442376 | tf_op jit(solution)/shard_map/ppermute | solution.py:805
  217.2 12.7 %collective-permute-start.19 = (bf16[16,8,768]{2,1,0:T(8,128)(2,1)S(1)}, bf16[16,8,768]{2,1,0:T(8,128)(2,1)S(1)}, u32[]{:S(2)}, u32[]{:S(2)}) collective-permute-start(bf16[16,8,768]{2,1,0:T(8,128)(2,1)S(1)} %add_convert_fusion.21), channel_id=1, source_target_pairs={{0,16},{1,17},{2,18},{3,19},{4,20},{5,21},{6,22},{7,23},{8,24},{9,... | collective-permute-start | bytes 589832 | tf_op jit(solution)/shard_map/ppermute | solution.py:805
